TPU v7x, 1024 devices: a whole 4x4x32 slice. The times are simulated.
1024 devices in a mesh: slab: 32 (over z_lo, y), grid: 32 (over x, z_hi, core).
Axes of the slice: x: 4, y: 4, z: 32 (z_hi: 4, z_lo: 8; z = z_hi * 8 + z_lo), core: 2. Of those that a mesh axis runs over, the one named last changes fastest.
Arguments:
- orbitals: bfloat16 [64, 110592], P(None, 'grid'), may hold values from -6 to 6
- targets: int32 [64], replicated, may hold values from 0 to 63
- points: int32 [1024], P('slab'), may hold values from 0 to 110591, as said below
- fit: float32 [1024, 32], P('slab'), may hold values from -2 to 4, as said below
Outputs:
- applied_exchange: float32 [64, 110592], P('slab', 'grid')
Inputs may be any that keep to these rules, and one draw needn't show every extreme that they name: `points`: 1024 distinct grid cells. `fit`: each block of 32 rows is a symmetric matrix.
All inputs are finite; a program needn't handle non-finite values.
Results may differ from a plain program's by a relative error of at most 0.004.
Values may be sent and summed in bfloat16 or wider, within the bound.
A program may use at most 32 MiB of HBM per device.

v0:
```python
import math

import jax
import jax.numpy as jnp
from jax import lax
from jax.sharding import PartitionSpec as P

NG = 48


screening = 4.0
careful = lax.Precision.HIGH


def dft_tables(length):
    positions = jnp.arange(length, dtype=jnp.int32)
    product = positions[:, None] * positions[None, :] % length
    angles = product.astype(jnp.float32) * (2.0 * math.pi / length)
    return (jnp.cos(angles), jnp.sin(angles))


def kernel_table():
    full_index = jnp.arange(NG, dtype=jnp.int32)
    wrapped = jnp.where(full_index > NG // 2, full_index - NG, full_index).astype(jnp.float32)
    half_index = jnp.arange(NG // 2 + 1, dtype=jnp.int32).astype(jnp.float32)
    step_size = 2.0 * math.pi / NG
    full_sq = wrapped * step_size * (wrapped * step_size)
    half_sq = half_index * step_size * (half_index * step_size)
    summed = full_sq[:, None, None] + full_sq[None, :, None] + half_sq[None, None, :]
    return screening / (screening + summed)


def apply_axis(values, matrix, pattern):
    return jnp.einsum(
        pattern, values, matrix, precision=careful, preferred_element_type=jnp.float32
    )


def split_apply(values, matrix, pattern):
    upper = matrix.astype(jnp.bfloat16)
    lower = (matrix - upper.astype(jnp.float32)).astype(jnp.bfloat16)
    first = jnp.einsum(pattern, values, upper, preferred_element_type=jnp.float32)
    return first + jnp.einsum(pattern, values, lower, preferred_element_type=jnp.float32)


def solve_one(vector_row):
    half_len = NG // 2 + 1
    cosine, sin_table = dft_tables(NG)
    cos_half = cosine[:, :half_len]
    sin_half = sin_table[:, :half_len]
    cube_vals = vector_row.reshape(NG, NG, NG)
    real_part = split_apply(cube_vals, cos_half, "xyz,zm->xym")
    imag_part = -split_apply(cube_vals, sin_half, "xyz,zm->xym")
    for pattern in ("xym,yb->xbm", "xym,xb->bym"):
        real_next = apply_axis(real_part, cosine, pattern) + apply_axis(
            imag_part, sin_table, pattern
        )
        imag_part = apply_axis(imag_part, cosine, pattern) - apply_axis(
            real_part, sin_table, pattern
        )
        real_part = real_next
    weights = kernel_table()
    real_part = real_part * weights
    imag_part = imag_part * weights
    for pattern in ("xym,xb->bym", "xym,yb->xbm"):
        real_next = apply_axis(real_part, cosine, pattern) - apply_axis(
            imag_part, sin_table, pattern
        )
        imag_part = apply_axis(real_part, sin_table, pattern) + apply_axis(
            imag_part, cosine, pattern
        )
        real_part = real_next
    frequency = jnp.arange(half_len, dtype=jnp.int32)
    fold_weight = jnp.where((frequency == 0) | (frequency == NG // 2), 1.0, 2.0).astype(jnp.float32)
    result = apply_axis(real_part * fold_weight, cos_half, "xym,zm->xyz") - apply_axis(
        imag_part * fold_weight, sin_half, "xym,zm->xyz"
    )
    return (result * (1.0 / (NG * NG * NG))).reshape(-1).astype(jnp.bfloat16)


def body(orbitals, targets, points, fit):
    occupied, shard_len = orbitals.shape
    target_count = targets.shape[0]
    group_size = points.shape[0]
    slab_count = lax.axis_size("slab")
    offsets = points - lax.axis_index("grid") * shard_len
    cell_ids = lax.broadcasted_iota(jnp.int32, (group_size, shard_len), 1)
    one_hot = (cell_ids == offsets[:, None]).astype(jnp.bfloat16)
    point_terms = lax.dot_general(
        orbitals, one_hot, (((1,), (1,)), ((), ())), preferred_element_type=jnp.float32
    )
    at_points = lax.psum(point_terms, "grid").astype(jnp.bfloat16)
    chosen = jnp.take(orbitals, targets, axis=0)
    target_points = jnp.take(at_points, targets, axis=0)
    contract_first = (((0,), (0,)), ((), ()))
    density = lax.dot_general(
        at_points, orbitals, contract_first, preferred_element_type=jnp.float32
    ) * (1.0 / math.sqrt(occupied))
    target_density = lax.dot_general(
        target_points, chosen, contract_first, preferred_element_type=jnp.float32
    ) * (1.0 / math.sqrt(target_count))
    pairs = density * target_density
    fitted = lax.dot_general(
        fit,
        pairs,
        contract_first,
        precision=lax.Precision.HIGHEST,
        preferred_element_type=jnp.float32,
    ).astype(jnp.bfloat16)
    vectors = lax.all_to_all(fitted, "grid", split_axis=0, concat_axis=1, tiled=True)
    potential = lax.map(solve_one, vectors)
    returned = lax.all_to_all(potential, "grid", split_axis=1, concat_axis=0, tiled=True)
    weighted = (returned.astype(jnp.float32) * density).astype(jnp.bfloat16)
    prefactor = -1.0 / math.sqrt(group_size * slab_count)
    summed = lax.psum_scatter(
        jnp.dot(target_points, weighted, preferred_element_type=jnp.float32),
        "slab",
        scatter_dimension=0,
        tiled=True,
    )
    return summed * prefactor


def solution(mesh):
    in_specs = (P(None, "grid"), P(), P("slab"), P("slab", None))
    out_specs = P("slab", "grid")
    return jax.shard_map(body, mesh=mesh, in_specs=in_specs, out_specs=out_specs, check_vma=False)
```

profile of v0, /device:TPU:6, one launch (start us, length us, event | category | flops | bytes accessed | tf_op | source)
XLA Modules:
  0.0 854.6 jit_solution(3439051326926051821)
XLA Ops:
  6.5 0.7 compare_and_fusion
  7.3 0.7 compare_select_fusion.1
  7.9 0.7 broadcast_subtract_fusion
  8.6 0.3 convolution_bitcast_fusion
  8.9 245.4 %psum.7 = bf16[64,32]{0,1:T(8,128)(2,1)S(1)} all-reduce(f32[64,32]{0,1:T(8,128)S(1)} %convolution_bitcast_fusion), channel_id=1, replica_groups=mesh['slab'=32,'grid'=32] {'grid'}, use_global_device_ids=true, to_apply=%region_0.0 | all-reduce | flops 2048 | bytes 12288 | tf_op jit(solution)/shard_map/psum | solution.py:92
  254.6 0.8 gather_fusion.1
  255.4 0.6 gather_fusion
  256.1 0.3 fusion
  256.4 0.6 fusion.1
  257.0 0.5 broadcast.193
  257.5 0.7 reduce.1
  258.2 0.9 reshape.142
  259.2 25.3 %all-to-all-start = ((bf16[32,2,1728]{2,1,0:T(2,128)(2,1)}), bf16[32,2,1728]{2,1,0:T(2,128)(2,1)S(1)}, u32[]{:S(2)}, u32[]{:S(2)}) async-start(bf16[32,2,1728]{2,1,0:T(2,128)(2,1)} %reshape.142), calls=%async_computation | async-start | bytes 458752 | tf_op jit(solution)/shard_map/all_to_all | solution.py:110
  285.0 33.1 %all-to-all-done = bf16[32,2,1728]{2,1,0:T(2,128)(2,1)S(1)} async-done(((bf16[32,2,1728]{2,1,0:T(2,128)(2,1)}), bf16[32,2,1728]{2,1,0:T(2,128)(2,1)S(1)}, u32[]{:S(2)}, u32[]{:S(2)}) %all-to-all-start) | async-done | bytes 221216 | tf_op jit(solution)/shard_map/all_to_all | solution.py:110
  318.2 0.3 reshape.143
  318.5 1.3 reduce
  319.7 0.5 reshape.108
  320.3 0.7 fusion.86
  321.0 0.8 fusion.8
  321.8 1.3 fusion.19
  323.1 0.7 fusion.88
  323.8 0.8 convolution_add_fusion.2
  324.6 1.3 fusion.23
  325.8 1.3 fusion.11
  327.1 1.3 fusion.12
  328.3 1.2 fusion.52
  329.5 1.2 fusion.47
  330.7 1.2 fusion.10
  331.8 0.5 fusion.38
  332.3 0.5 fusion.49
  332.8 1.2 fusion.9
  334.0 0.7 convolution_subtract_fusion.2
  334.8 0.7 fusion.15
  335.5 0.7 fusion.17
  336.2 0.5 convolution_add_fusion.3
  336.7 0.7 fusion.7
  337.4 0.7 fusion.5
  338.1 1.1 fusion.62
  339.2 1.2 fusion.3
  340.4 0.8 convert_element_type.150
  341.2 2.0 reduce.2
  343.2 0.3 reshape.144
  343.4 43.6 %all_to_all.23 = bf16[32,2,1728]{2,1,0:T(2,128)(2,1)S(1)} all-to-all(bf16[32,2,1728]{2,1,0:T(2,128)(2,1)S(1)} %reshape.144), channel_id=1, replica_groups=mesh['slab'=32,'grid'=32] {'grid'}, dimensions={0} | all-to-all | bytes 442368 | tf_op jit(solution)/shard_map/all_to_all | solution.py:112
  387.1 0.3 reshape.145
  387.4 1.3 fusion.28
  388.7 1.3 dynamic-slice
  390.6 455.6 %all-reduce.3.cloned.1.call-done = f32[64,3456]{1,0:T(8,128)} async-done(((f32[64,3456]{1,0:T(8,128)}), f32[64,3456]{1,0:T(8,128)}) %all-reduce.3.cloned.1.call-update) | async-done | bytes 884752
  846.2 1.5 dynamic-slice_multiply_fusion
  (15 shorter events, 0.9 us)
Async XLA Ops:
  6.5 2.0 copy-start
  255.4 1.0 copy-start.1
  259.2 59.0 %all-to-all-start = ((bf16[32,2,1728]{2,1,0:T(2,128)(2,1)}), bf16[32,2,1728]{2,1,0:T(2,128)(2,1)S(1)}, u32[]{:S(2)}, u32[]{:S(2)}) async-start(bf16[32,2,1728]{2,1,0:T(2,128)(2,1)} %reshape.142), calls=%async_computation | async-start | bytes 458752 | tf_op jit(solution)/shard_map/all_to_all | solution.py:110
  284.5 561.7 %all-reduce.3.cloned.1.call-start = ((), (), s32[]{:S(2)}) async-start(), calls=%async_computation.2 | async-start | bytes 1769472
Sparse Core Ops, SparseCore 0:
  388.8 457.3 all-reduce.2
where the time goes:
time: 856 us; the launch traced here: 855 us
  waiting for transfers between devices  489 us (57%)
  blocking collectives  289 us (34%)
  starting transfers between devices  25.5 us (3%)
  matrix products  22.6 us (3%)
  between operations  14.3 us (2%)
    unnamed x2, waiting for transfers between devices  456 us
    psum x1, blocking collectives, body(): at_points = lax.psum(point_terms, 'grid').astype(jnp.bfloat16)  245 us
    all_to_all x1, blocking collectives, body(): lax.all_to_all(potential, 'grid', split_axis=1, concat_axis=0, tiled=True)  43.6 us
    all_to_all x1, waiting for transfers between devices, body(): lax.all_to_all(fitted, 'grid', split_axis=0, concat_axis=1, tiled=True)  33.1 us
    all_to_all x1, starting transfers between devices, body(): lax.all_to_all(fitted, 'grid', split_axis=0, concat_axis=1, tiled=True)  25.3 us
  transfers between devices with their start and end apart: 2, of which 2 were waited for; matrix products, arithmetic and copies ran while one was open for 0% of the time, Pallas kernels for 0%

commit v1 on v0

v1 whole, which is shorter than its diff:
```python
import functools
import math

import jax
import jax.numpy as jnp
import numpy as np
from jax import lax
from jax.experimental import pallas as pl
from jax.experimental.pallas import tpu as pltpu
from jax.sharding import PartitionSpec as P

NG = 48
SCREENING = 4.0
MESH = pl.DeviceIdType.MESH
N_X, N_HI, N_CORE = 4, 4, 2
N_LO, N_Y = 8, 4
LANES = 128


def real_basis():
    rows, freq = [], []
    place = np.arange(NG)
    for m in range(NG // 2 + 1):
        scale = math.sqrt((1.0 if m in (0, NG // 2) else 2.0) / NG)
        rows.append(scale * np.cos(2.0 * math.pi * m * place / NG))
        freq.append(m)
    for m in range(1, NG // 2):
        rows.append(math.sqrt(2.0 / NG) * np.sin(2.0 * math.pi * m * place / NG))
        freq.append(m)
    return np.array(rows), np.array(freq)


BASIS, FREQ = real_basis()


def multiplier():
    sq = (2.0 * math.pi * FREQ / NG) ** 2
    return SCREENING / (SCREENING + sq[:, None, None] + sq[None, :, None] + sq[None, None, :])


def solve(vector):
    basis = jnp.asarray(BASIS, jnp.float32)
    weights = jnp.asarray(multiplier(), jnp.float32)
    cube = vector.reshape(NG, NG, NG).astype(jnp.float32)
    for pattern in ("xyz,mz->xym", "xyz,my->xmz", "xyz,mx->myz"):
        cube = jnp.einsum(pattern, cube, basis, precision=lax.Precision.HIGH)
    cube = cube * weights
    for pattern in ("myz,mx->xyz", "xmz,my->xyz", "xym,mz->xyz"):
        cube = jnp.einsum(pattern, cube, basis, precision=lax.Precision.HIGH)
    return cube.reshape(-1)


def greet(peers):
    barrier = pltpu.get_barrier_semaphore()
    for peer in peers:
        pl.semaphore_signal(barrier, inc=1, device_id=peer, device_id_type=MESH)
    pl.semaphore_wait(barrier, len(peers))


def push(src, dst, send, recv, peer):
    copy = pltpu.make_async_remote_copy(
        src_ref=src, dst_ref=dst, send_sem=send, recv_sem=recv, device_id=peer, device_id_type=MESH
    )
    copy.start()
    return copy


def points_kernel(mine_ref, out_ref, near, part, far, near_send, near_recv, far_send, far_recv):
    g = lax.axis_index("grid")
    core = lax.rem(g, N_CORE)
    hi = lax.rem(g // N_CORE, N_HI)
    x = g // (N_CORE * N_HI)

    def near_peer(dx, dc):
        return ((lax.rem(x + dx, N_X)) * N_HI + hi) * N_CORE + lax.rem(core + dc, N_CORE)

    def far_peer(dh):
        return (x * N_HI + lax.rem(hi + dh, N_HI)) * N_CORE + core

    near_steps = [(dx, dc) for dx in range(N_X) for dc in range(N_CORE) if dx or dc]
    greet([{"grid": near_peer(*step)} for step in near_steps] + [{"grid": far_peer(dh)} for dh in range(1, N_HI)])
    copies = [
        push(mine_ref, near.at[i], near_send.at[i], near_recv.at[i], {"grid": near_peer(*step)})
        for i, step in enumerate(near_steps)
    ]
    for copy in copies:
        copy.wait()
    total = mine_ref[...].astype(jnp.float32)
    for i in range(len(near_steps)):
        total = total + near[i].astype(jnp.float32)
    part[...] = total.astype(jnp.bfloat16)
    copies = [
        push(part, far.at[dh - 1], far_send.at[dh - 1], far_recv.at[dh - 1], {"grid": far_peer(dh)})
        for dh in range(1, N_HI)
    ]
    for copy in copies:
        copy.wait()
    for i in range(N_HI - 1):
        total = total + far[i].astype(jnp.float32)
    out_ref[...] = total.astype(jnp.bfloat16)


VMEM_SPEC = pl.BlockSpec(memory_space=pltpu.VMEM)


def sum_points(mine):
    near = N_X * N_CORE - 1
    far = N_HI - 1
    return pl.pallas_call(
        points_kernel,
        out_shape=jax.ShapeDtypeStruct(mine.shape, mine.dtype),
        in_specs=[VMEM_SPEC],
        out_specs=VMEM_SPEC,
        scratch_shapes=[
            pltpu.VMEM((near,) + mine.shape, mine.dtype),
            pltpu.VMEM(mine.shape, mine.dtype),
            pltpu.VMEM((far,) + mine.shape, mine.dtype),
            pltpu.SemaphoreType.DMA((near,)),
            pltpu.SemaphoreType.DMA((near,)),
            pltpu.SemaphoreType.DMA((far,)),
            pltpu.SemaphoreType.DMA((far,)),
        ],
        compiler_params=pltpu.CompilerParams(collective_id=0, has_side_effects=True),
        name="sum_points",
    )(mine)


def exchange_kernel(axis, n, stride, src_ref, out_ref, send, recv, local):
    index = lax.axis_index(axis)
    me = lax.rem(index // stride, n)
    base = index - me * stride

    def peer(d):
        return {axis: base + lax.rem(me + d, n) * stride}

    barrier = pltpu.get_barrier_semaphore()

    def hello(d, carry):
        pl.semaphore_signal(barrier, inc=1, device_id=peer(d), device_id_type=MESH)
        return carry

    lax.fori_loop(1, n, hello, 0)
    own = pltpu.make_async_copy(src_ref.at[me], out_ref.at[me], local)
    own.start()
    pl.semaphore_wait(barrier, n - 1)

    def describe(d):
        return pltpu.make_async_remote_copy(
            src_ref=src_ref.at[lax.rem(me + d, n)],
            dst_ref=out_ref.at[me],
            send_sem=send.at[d],
            recv_sem=recv.at[d],
            device_id=peer(d),
            device_id_type=MESH,
        )

    def begin(d, carry):
        describe(d).start()
        return carry

    def finish(d, carry):
        copy = describe(d)
        copy.wait_send()
        copy.wait_recv()
        return carry

    lax.fori_loop(1, n, begin, 0)
    own.wait()
    lax.fori_loop(1, n, finish, 0)


def exchange(blocks, axis, n, stride, ident, name):
    return pl.pallas_call(
        functools.partial(exchange_kernel, axis, n, stride),
        out_shape=jax.ShapeDtypeStruct(blocks.shape, blocks.dtype),
        in_specs=[VMEM_SPEC],
        out_specs=VMEM_SPEC,
        scratch_shapes=[
            pltpu.SemaphoreType.DMA((n,)),
            pltpu.SemaphoreType.DMA((n,)),
            pltpu.SemaphoreType.DMA,
        ],
        compiler_params=pltpu.CompilerParams(collective_id=ident, has_side_effects=True),
        name=name,
    )(blocks)


def body(orbitals, targets, points, fit):
    occupied, shard_len = orbitals.shape
    target_count = targets.shape[0]
    group_size = points.shape[0]
    n_grid = N_X * N_HI * N_CORE
    slab_count = N_LO * N_Y
    tiles = shard_len // LANES
    rows_each = target_count // slab_count
    offsets = points - lax.axis_index("grid") * shard_len
    cell_ids = lax.broadcasted_iota(jnp.int32, (group_size, shard_len), 1)
    one_hot = (cell_ids == offsets[:, None]).astype(jnp.bfloat16)
    terms = lax.dot_general(
        one_hot, orbitals, (((1,), (1,)), ((), ())), preferred_element_type=jnp.float32
    ).astype(jnp.bfloat16)
    at_points = sum_points(terms)
    choose = (lax.broadcasted_iota(jnp.int32, (occupied, target_count), 0) == targets[None, :]).astype(jnp.bfloat16)
    target_points = jnp.dot(at_points, choose, preferred_element_type=jnp.float32).astype(jnp.bfloat16)
    density = jnp.dot(at_points, orbitals, preferred_element_type=jnp.float32) * (1.0 / math.sqrt(occupied))
    chosen = lax.dot_general(
        choose, orbitals, (((0,), (0,)), ((), ())), preferred_element_type=jnp.float32
    ).astype(jnp.bfloat16)
    target_density = jnp.dot(target_points, chosen, preferred_element_type=jnp.float32) * (
        1.0 / math.sqrt(target_count)
    )
    pairs = density * target_density
    fitted = lax.dot_general(
        fit, pairs, (((0,), (0,)), ((), ())), precision=lax.Precision.HIGHEST, preferred_element_type=jnp.float32
    ).astype(jnp.bfloat16)
    vectors = exchange(fitted.reshape(n_grid, tiles, LANES), "grid", n_grid, 1, 1, "spread")
    potential = solve(vectors).astype(jnp.bfloat16)
    returned = exchange(potential.reshape(n_grid, tiles, LANES), "grid", n_grid, 1, 2, "collect")
    returned = returned.reshape(group_size, shard_len)
    weighted = (returned.astype(jnp.float32) * density).astype(jnp.bfloat16)
    ordered = target_points.reshape(group_size, N_LO, N_Y, rows_each).transpose(0, 2, 1, 3).reshape(group_size, -1)
    partial = lax.dot_general(
        ordered, weighted, (((0,), (0,)), ((), ())), preferred_element_type=jnp.float32
    ).astype(jnp.bfloat16)
    by_y = exchange(partial.reshape(N_Y, -1, shard_len), "slab", N_Y, 1, 3, "sum_y")
    half = jnp.sum(by_y.astype(jnp.float32), axis=0).astype(jnp.bfloat16)
    by_lo = exchange(half.reshape(N_LO, rows_each * tiles, LANES), "slab", N_LO, N_Y, 4, "sum_lo")
    summed = jnp.sum(by_lo.astype(jnp.float32), axis=0).reshape(rows_each, shard_len)
    return summed * (-1.0 / math.sqrt(group_size * slab_count))


def solution(mesh):
    in_specs = (P(None, "grid"), P(), P("slab"), P("slab", None))
    out_specs = P("slab", "grid")
    return jax.shard_map(body, mesh=mesh, in_specs=in_specs, out_specs=out_specs, check_vma=False)
```

time: 856 us -> 176 us (0.21)
  waiting for transfers between devices: 489 us -> 0 us
  blocking collectives: 289 us -> 0 us
  Pallas kernels: 0 us -> 155 us
  starting transfers between devices: 25.5 us -> 0 us
  between operations: 14.3 us -> 0.2 us
  matrix products: 22.6 us -> 9.55 us
    unnamed x2 -> x0, waiting for transfers between devices: 456 us -> none
    psum x1 -> x0, blocking collectives: 245 us -> none  [body(): at_points = lax.psum(point_terms, 'grid').astype(jnp.bfloat16)]
    pallas_call x0 -> x5, Pallas kernels: none -> 155 us  [the longest x4 115 us: exchange(): pl.pallas_call(functools.partial(exchange_kernel, axis, n, stride), out_s...]
    all_to_all x1 -> x0, blocking collectives: 43.6 us -> none  [body(): lax.all_to_all(potential, 'grid', split_axis=1, concat_axis=0, tiled=True)]
    all_to_all x1 -> x0, waiting for transfers between devices: 33.1 us -> none  [body(): lax.all_to_all(fitted, 'grid', split_axis=0, concat_axis=1, tiled=True)]
    all_to_all x1 -> x0, starting transfers between devices: 25.3 us -> none  [body(): lax.all_to_all(fitted, 'grid', split_axis=0, concat_axis=1, tiled=True)]
    dot_general x27 -> x12, matrix products: 22.6 us -> 9.55 us  [the longest x6 4.73 us: solve(): cube = jnp.einsum(pattern, cube, basis, precision=lax.Precision.HIGH)]
  transfers between devices with their start and end apart: 2 -> 0, of which waited for: 2 -> 0; matrix products, arithmetic and copies ran while one was open for 0% -> 0% of each run, Pallas kernels for 0% -> 0%
where the time goes in v1:
time: 176 us; the launch traced here: 175 us
  Pallas kernels  155 us (88%)
  matrix products  9.55 us (5%)
  local copies, waits for them, and re-layouts  6.54 us (4%)
  other arithmetic  4.2 us (2%)
    pallas_call x4, Pallas kernels, exchange(): pl.pallas_call(functools.partial(exchange_kernel, axis, n, stride), out_s...  115 us
    pallas_call x1, Pallas kernels, sum_points(): pl.pallas_call(points_kernel, out_shape=jax.ShapeDtypeStruct(mine.shape,...  39.1 us
    dot_general x6, matrix products, solve(): cube = jnp.einsum(pattern, cube, basis, precision=lax.Precision.HIGH)  4.73 us

profile of v1, /device:TPU:6, one launch (start us, length us, event | category | flops | bytes accessed | tf_op | source)
XLA Modules:
  0.0 175.1 jit_solution(15814516050462105866)
XLA Ops:
  0.0 0.0 copy-start
  0.0 0.0 copy-start.4
  0.0 0.7 broadcast_subtract_fusion
  0.7 0.3 copy-done
  1.0 0.9 convolution_convert_fusion.5.mine_ref
  1.9 0.0 copy-start.3
  1.9 39.1 %sum_points.1 = bf16[32,64]{1,0:T(8,128)(2,1)} custom-call(bf16[32,64]{1,0:T(8,128)(2,1)} %convolution_convert_fusion.5.mine_ref), custom_call_target="tpu_custom_call" | custom-call | tf_op jit(solution)/shard_map/sum_points/pallas_call | solution.py:109
  41.1 0.9 convolution_multiply_fusion.1
  42.0 0.0 copy-done.4
  42.0 0.8 convolution_convert_fusion.4
  42.8 0.5 fusion
  43.3 0.0 copy-done.3
  43.3 0.0 copy-start.2
  43.3 0.6 fusion.1
  43.9 0.8 reshape.32.src_ref
  44.7 41.6 %spread.1 = bf16[32,27,128]{2,1,0:T(8,128)(2,1)} custom-call(bf16[32,27,128]{2,1,0:T(8,128)(2,1)} %reshape.32.src_ref), custom_call_target="tpu_custom_call" | custom-call | tf_op jit(solution)/shard_map/spread/pallas_call | solution.py:173
  86.3 1.5 reshape.33
  87.8 0.0 copy-done.2
  87.8 0.5 fusion.11
  88.3 1.1 convolution_bitcast_fusion.1
  89.4 0.6 copy.9
  89.9 0.0 copy-start.1
  89.9 0.6 fusion.12
  90.6 0.6 copy-done.1
  91.2 0.5 copy_multiply_fusion
  91.7 1.0 fusion.3
  92.7 1.0 convolution_bitcast_fusion
  93.6 0.6 convolution_convert_fusion.3
  94.3 1.2 convert_element_type.48.src_ref
  95.4 38.9 %collect.1 = bf16[32,27,128]{2,1,0:T(8,128)(2,1)} custom-call(bf16[32,27,128]{2,1,0:T(8,128)(2,1)} %convert_element_type.48.src_ref), custom_call_target="tpu_custom_call" | custom-call | tf_op jit(solution)/shard_map/collect/pallas_call | solution.py:173
  134.4 1.0 convert.2
  135.4 0.1 copy.7
  135.5 1.2 convolution_convert_fusion
  136.7 20.1 %sum_y.1 = bf16[4,16,3456]{2,1,0:T(8,128)(2,1)} custom-call(bf16[4,16,3456]{2,1,0:T(8,128)(2,1)} %bitcast.38), custom_call_target="tpu_custom_call" | custom-call | tf_op jit(solution)/shard_map/sum_y/pallas_call | solution.py:173
  156.8 1.1 reduce_sum.21
  157.9 0.8 reshape.35.src_ref
  158.7 14.9 %sum_lo.1 = bf16[8,54,128]{2,1,0:T(8,128)(2,1)} custom-call(bf16[8,54,128]{2,1,0:T(8,128)(2,1)} %reshape.35.src_ref), custom_call_target="tpu_custom_call" | custom-call | tf_op jit(solution)/shard_map/sum_lo/pallas_call | solution.py:173
  173.5 0.9 convert_reduce_fusion
  174.5 0.6 mul.35
  (2 shorter events, 0.0 us)
Async XLA Ops:
  0.0 1.0 copy-start
  0.0 42.0 %copy-start.4 = (s32[64]{0:T(128)S(1)}, s32[64]{0:T(128)}, u32[]{:S(2)}) copy-start(s32[64]{0:T(128)} %param.7) | copy-start | bytes 772
  1.9 41.4 %copy-start.3 = (f32[32,32]{1,0:T(8,128)S(1)}, f32[32,32]{1,0:T(8,128)}, u32[]{:S(2)}) copy-start(f32[32,32]{1,0:T(8,128)} %param.9) | copy-start | bytes 12292
  43.3 44.5 %copy-start.2 = (f32[48,48,1]{1,0,2:T(8,128)S(1)}, f32[48,48,1]{1,0,2:T(8,128)}, u32[]{:S(2)}) copy-start(f32[48,48,1]{1,0,2:T(8,128)} %constant.20) | copy-start | bytes 27652
  89.9 1.3 copy-start.1

commit v2 on v0

v2 whole, which is shorter than its diff:
```python
import functools
import math

import jax
import jax.numpy as jnp
import numpy as np
from jax import lax
from jax.experimental import pallas as pl
from jax.experimental.pallas import tpu as pltpu
from jax.sharding import PartitionSpec as P

NG = 48
SCREENING = 4.0
MESH = pl.DeviceIdType.MESH
N_X, N_HI, N_CORE = 4, 4, 2
N_LO, N_Y = 8, 4
N_GRID = N_X * N_HI * N_CORE
LANES = 128
SLOT = 32
F32, BF16 = jnp.float32, jnp.bfloat16


def real_basis():
    rows, freq = [], []
    place = np.arange(NG)
    for m in range(NG // 2 + 1):
        scale = math.sqrt((1.0 if m in (0, NG // 2) else 2.0) / NG)
        rows.append(scale * np.cos(2.0 * math.pi * m * place / NG))
        freq.append(m)
    for m in range(1, NG // 2):
        rows.append(math.sqrt(2.0 / NG) * np.sin(2.0 * math.pi * m * place / NG))
        freq.append(m)
    return np.array(rows), np.array(freq)


def split_table(table):
    high = table.astype(BF16)
    low = (table - high.astype(np.float64)).astype(BF16)
    return high, low


def tables():
    basis, freq = real_basis()
    left = []
    for matrix in (basis, basis.T):
        high, low = split_table(matrix)
        left.append(np.concatenate([high, high, low], axis=1))
    lines = np.zeros((2 * NG, LANES), BF16)
    high, low = split_table(basis.T)
    lines[:NG, :NG] = high
    lines[NG:, :NG] = low
    square = ((2.0 * math.pi * freq / NG) ** 2).astype(np.float32)
    column = np.broadcast_to(square[:, None], (NG, LANES)).copy()
    row = np.zeros((8, LANES), np.float32)
    row[:, :NG] = square
    return np.stack(left), lines, np.concatenate([column, row])


def stack(values):
    high = values.astype(BF16)
    low = (values - high.astype(F32)).astype(BF16)
    return jnp.concatenate([high, low, high], axis=0)


def dot(a, b):
    return jnp.dot(a, b, preferred_element_type=F32)


def dot_nt(a, b):
    return lax.dot_general(a, b, (((1,), (1,)), ((), ())), preferred_element_type=F32)


def column_of(row, count):
    same = lax.broadcasted_iota(jnp.int32, (count, count), 0) == lax.broadcasted_iota(jnp.int32, (count, count), 1)
    return jnp.sum(jnp.where(same, row, 0), axis=1, keepdims=True)


def spans(line):
    return range(line * NG // LANES, (line * NG + NG - 1) // LANES + 1)


def kernel(
    occupied, targets_n, group, shard, orb_ref, targets_ref, points_ref, fit_ref, left_ref, lines_ref, square_ref,
    out_ref, mine, near, part, far, chosen, density, flat, packed, cells, cube, weights, zline,
    send_a, recv_a, send_b, recv_b, y_out, y_in, lo_flat, lo_out, lo_in, last,
    near_s, near_r, far_s, far_r, a_s, a_r, b_s, b_r, y_s, y_r, lo_s, lo_r, local,
):
    grid, slab = lax.axis_index("grid"), lax.axis_index("slab")
    core, hi, x = lax.rem(grid, N_CORE), lax.rem(grid // N_CORE, N_HI), grid // (N_CORE * N_HI)
    lo, y = slab // N_Y, lax.rem(slab, N_Y)
    tiles = shard // LANES
    rows = tiles // 3
    wire = tiles + tiles % 2
    each = targets_n // (N_LO * N_Y)

    def grid_peer(dx, dh, dc):
        return (lax.rem(x + dx, N_X) * N_HI + lax.rem(hi + dh, N_HI)) * N_CORE + lax.rem(core + dc, N_CORE)

    def y_peer(d):
        return lo * N_Y + lax.rem(y + d, N_Y)

    def lo_peer(d):
        return lax.rem(lo + d, N_LO) * N_Y + y

    offsets = [(dx, dh, dc) for dh in (2, 1, 3, 0) for dx in range(N_X) for dc in range(N_CORE) if dx or dh or dc]
    barrier = pltpu.get_barrier_semaphore()
    for step in offsets:
        pl.semaphore_signal(barrier, inc=1, device_id={"grid": grid_peer(*step)}, device_id_type=MESH)
    for d in range(1, N_Y):
        pl.semaphore_signal(barrier, inc=1, device_id={"slab": y_peer(d)}, device_id_type=MESH)
    for d in range(1, N_LO):
        pl.semaphore_signal(barrier, inc=1, device_id={"slab": lo_peer(d)}, device_id_type=MESH)

    def push(src, dst, send, recv, peer):
        copy = pltpu.make_async_remote_copy(
            src_ref=src, dst_ref=dst, send_sem=send, recv_sem=recv, device_id=peer, device_id_type=MESH
        )
        copy.start()
        return copy

    offset = column_of(points_ref[...], group) - grid * shard
    for i in range(rows):
        ids = lax.broadcasted_iota(jnp.int32, (group, 384), 1) + i * 384
        term = dot_nt(
            jnp.where(ids == offset, 1.0, 0.0).astype(BF16), orb_ref[:, i * 384 : (i + 1) * 384]
        )
        total = term if i == 0 else total + term
    mine[...] = total.astype(BF16)
    targets = targets_ref[...]
    occ = lax.broadcasted_iota(jnp.int32, (occupied, targets_n), 0)
    choose = jnp.where(occ == targets, 1.0, 0.0).astype(BF16)
    pick = jnp.where(
        lax.broadcasted_iota(jnp.int32, (targets_n, occupied), 1) == column_of(targets, targets_n), 1.0, 0.0
    ).astype(BF16)
    new = lax.broadcasted_iota(jnp.int32, (targets_n, targets_n), 0)
    old = lax.broadcasted_iota(jnp.int32, (targets_n, targets_n), 1)
    from_old = ((new // each) % N_LO) * (N_Y * each) + (new // (each * N_LO)) * each + new % each
    reorder = dot(jnp.where(old == from_old, 1.0, 0.0).astype(BF16), pick).astype(BF16)
    for i in range(rows):
        chosen[:, i * 384 : (i + 1) * 384] = dot(pick, orb_ref[:, i * 384 : (i + 1) * 384]).astype(BF16)
    zline[...] = jnp.zeros_like(zline)
    for line in range(8):
        at = slice(line * NG, (line + 1) * NG)
        for k in range(2):
            zline[k, at, line * LANES : (line + 1) * LANES] = lines_ref[k * NG : (k + 1) * NG, :]
    flat[...] = jnp.zeros_like(flat)
    lo_flat[...] = jnp.zeros_like(lo_flat)
    column, row = square_ref[:NG, :], square_ref[NG : NG + 1, :]

    def weigh(m, carry):
        one = square_ref[pl.ds(m, 1), :]
        weights[pl.ds(pl.multiple_of(m * NG, NG), NG), :] = SCREENING / (SCREENING + column + row + one[:, :1])
        return carry

    lax.fori_loop(0, NG, weigh, 0)
    fit = fit_ref[...]
    fit_1 = fit.astype(BF16)
    fit_2 = (fit - fit_1.astype(F32)).astype(BF16)
    fit_3 = (fit - fit_1.astype(F32) - fit_2.astype(F32)).astype(BF16)
    fits = jnp.concatenate([fit_1, fit_1, fit_2, fit_1, fit_2, fit_3], axis=1)

    pl.semaphore_wait(barrier, len(offsets) + N_Y - 1 + N_LO - 1)

    near_steps = [(dx, 0, dc) for dx in range(N_X) for dc in range(N_CORE) if dx or dc]
    copies = [
        push(mine, near.at[i], near_s.at[i], near_r.at[i], {"grid": grid_peer(*step)})
        for i, step in enumerate(near_steps)
    ]
    for copy in copies:
        copy.wait()
    total = mine[...].astype(F32)
    for i in range(len(near_steps)):
        total = total + near[i].astype(F32)
    part[...] = total.astype(BF16)
    copies = [
        push(part, far.at[d - 1], far_s.at[d - 1], far_r.at[d - 1], {"grid": grid_peer(0, d, 0)})
        for d in range(1, N_HI)
    ]
    for copy in copies:
        copy.wait()
    for i in range(N_HI - 1):
        total = total + far[i].astype(F32)
    at_points = total.astype(BF16)

    target_points = dot(at_points, choose).astype(BF16)
    ordered = dot_nt(reorder, at_points).astype(BF16)
    for i in range(rows):
        at = slice(i * 384, (i + 1) * 384)
        dense = dot(at_points, orb_ref[:, at]) * (1.0 / math.sqrt(occupied))
        density[:, at] = dense
        pair = dense * (dot(target_points, chosen[:, at]) * (1.0 / math.sqrt(targets_n)))
        pair_1 = pair.astype(BF16)
        rest = pair - pair_1.astype(F32)
        pair_2 = rest.astype(BF16)
        pair_3 = (rest - pair_2.astype(F32)).astype(BF16)
        fitted = dot(fits, jnp.concatenate([pair_1, pair_2, pair_1, pair_3, pair_2, pair_1], axis=0))
        for t in range(3):
            flat[pl.ds(3 * i + t, group, stride=SLOT), :] = fitted[:, t * LANES : (t + 1) * LANES]
    send_a[...] = flat[...].reshape(N_GRID, SLOT, LANES).astype(BF16)

    def spread(source, target, send, recv):
        own = pltpu.make_async_copy(source.at[grid], target.at[grid], local)
        own.start()
        copies = []
        for i, step in enumerate(offsets):
            peer = grid_peer(*step)
            copies.append(
                push(
                    source.at[peer, pl.ds(0, wire)], target.at[grid, pl.ds(0, wire)], send.at[i], recv.at[i],
                    {"grid": peer},
                )
            )
        own.wait()
        for copy in copies:
            copy.wait()
        flat[...] = target[...].astype(F32).reshape(N_GRID * SLOT, LANES)

    spread(send_a, recv_a, a_s, a_r)

    for i in range(rows):
        for t in range(3):
            packed[i * N_GRID : (i + 1) * N_GRID, t * LANES : (t + 1) * LANES] = flat[
                pl.ds(3 * i + t, N_GRID, stride=SLOT), :
            ].astype(BF16)
    for line in range(8):
        at = slice(line * LANES, (line + 1) * LANES)
        got = None
        for t in spans(line):
            lanes = slice(t * LANES, (t + 1) * LANES)
            for k in range(2):
                term = dot(packed[:, lanes], zline[k, lanes, at])
                got = term if got is None else got + term
        for i in range(rows):
            cube[pl.ds(8 * i + line, N_GRID, stride=8 * rows), :] = got[i * N_GRID : (i + 1) * N_GRID, :]

    many = 8

    def along_y(which):
        def one(step, carry):
            for u in range(0, many, 2):
                first = pl.ds(pl.multiple_of((step * many + u) * NG, NG), NG)
                second = pl.ds(pl.multiple_of((step * many + u + 1) * NG, NG), NG)
                both = jnp.concatenate([stack(cube[first, :]), stack(cube[second, :])], axis=1)
                got = dot(left_ref[which], both)
                cube[first, :] = got[:, :LANES]
                cube[second, :] = got[:, LANES:]
            return carry

        lax.fori_loop(0, NG // many, one, 0)

    def along_x(step, carry):
        for u in range(0, many, 2):
            first, second = step * many + u, step * many + u + 1
            at = [pl.ds(m, NG, stride=NG) for m in (first, second)]
            both = jnp.concatenate([stack(cube[at[0], :]), stack(cube[at[1], :])], axis=1)
            got = dot(left_ref[0], both)
            got = [
                got[:, k * LANES : (k + 1) * LANES] * weights[pl.ds(pl.multiple_of(m * NG, NG), NG), :]
                for k, m in enumerate((first, second))
            ]
            got = dot(left_ref[1], jnp.concatenate([stack(got[0]), stack(got[1])], axis=1))
            cube[at[0], :] = got[:, :LANES]
            cube[at[1], :] = got[:, LANES:]
        return carry

    along_y(0)
    lax.fori_loop(0, NG // many, along_x, 0)
    along_y(1)
    tile = [None, None, None]
    for line in range(8):
        at = slice(line * LANES, (line + 1) * LANES)
        for i in range(rows):
            cells[i * N_GRID : (i + 1) * N_GRID, :] = cube[pl.ds(8 * i + line, N_GRID, stride=8 * rows), :]
        value = cells[...]
        high = value.astype(BF16)
        low = (value - high.astype(F32)).astype(BF16)
        for t in spans(line):
            lanes = slice(t * LANES, (t + 1) * LANES)
            term = dot_nt(high, zline[0, lanes, at]) + dot_nt(low, zline[0, lanes, at])
            term = term + dot_nt(high, zline[1, lanes, at])
            tile[t] = term if tile[t] is None else tile[t] + term
    for i in range(rows):
        for t in range(3):
            flat[pl.ds(3 * i + t, N_GRID, stride=SLOT), :] = tile[t][i * N_GRID : (i + 1) * N_GRID, :]
    send_b[...] = flat[...].reshape(N_GRID, SLOT, LANES).astype(BF16)

    spread(send_b, recv_b, b_s, b_r)

    for i in range(rows):
        at = slice(i * 384, (i + 1) * 384)
        got = jnp.concatenate([flat[pl.ds(3 * i + t, group, stride=SLOT), :] for t in range(3)], axis=1)
        weighted = (got * density[:, at]).astype(BF16)
        y_out[:, :, at] = dot(ordered, weighted).astype(BF16).reshape(N_Y, targets_n // N_Y, 384)
    copies = [
        push(y_out.at[lax.rem(y + d, N_Y)], y_in.at[d - 1], y_s.at[d - 1], y_r.at[d - 1], {"slab": y_peer(d)})
        for d in range(1, N_Y)
    ]
    for copy in copies:
        copy.wait()
    for i in range(rows):
        at = slice(i * 384, (i + 1) * 384)
        total = y_out[y, :, at].astype(F32)
        for d in range(N_Y - 1):
            total = total + y_in[d, :, at].astype(F32)
        for t in range(3):
            lo_flat[pl.ds(3 * i + t, N_LO * each, stride=SLOT), :] = total[:, t * LANES : (t + 1) * LANES]
    lo_out[...] = lo_flat[...].reshape(N_LO, each, SLOT, LANES).astype(BF16)
    copies = [
        push(
            lo_out.at[lax.rem(lo + d, N_LO), :, pl.ds(0, wire)], lo_in.at[d - 1, :, pl.ds(0, wire)],
            lo_s.at[d - 1], lo_r.at[d - 1], {"slab": lo_peer(d)},
        )
        for d in range(1, N_LO)
    ]
    for copy in copies:
        copy.wait()
    total = lo_out[lo].astype(F32)
    for d in range(N_LO - 1):
        total = total + lo_in[d].astype(F32)
    last[...] = (total * (-1.0 / math.sqrt(group * N_LO * N_Y))).reshape(each * SLOT, LANES)
    for c in range(tiles):
        out_ref[:, c * LANES : (c + 1) * LANES] = last[pl.ds(c, each, stride=SLOT), :]


def body(orbitals, targets, points, fit):
    occupied, shard = orbitals.shape
    targets_n, group = targets.shape[0], points.shape[0]
    each = targets_n // (N_LO * N_Y)
    left, lines, square = tables()
    near, far = N_X * N_CORE - 1, N_HI - 1
    peers = N_GRID - 1
    dma = pltpu.SemaphoreType.DMA
    vmem = pltpu.VMEM
    return pl.pallas_call(
        functools.partial(kernel, occupied, targets_n, group, shard),
        out_shape=jax.ShapeDtypeStruct((each, shard), F32),
        in_specs=[pl.BlockSpec(memory_space=pltpu.VMEM)] * 7,
        out_specs=pl.BlockSpec(memory_space=pltpu.VMEM),
        scratch_shapes=[
            vmem((group, occupied), BF16),
            vmem((near, group, occupied), BF16),
            vmem((group, occupied), BF16),
            vmem((far, group, occupied), BF16),
            vmem((targets_n, shard), BF16),
            vmem((group, shard), F32),
            vmem((N_GRID * SLOT, LANES), F32),
            vmem((N_GRID * shard // 384, 384), BF16),
            vmem((N_GRID * shard // 384, LANES), F32),
            vmem((NG * NG, LANES), F32),
            vmem((NG * NG, LANES), F32),
            vmem((2, 384, 8 * LANES), BF16),
            vmem((N_GRID, SLOT, LANES), BF16),
            vmem((N_GRID, SLOT, LANES), BF16),
            vmem((N_GRID, SLOT, LANES), BF16),
            vmem((N_GRID, SLOT, LANES), BF16),
            vmem((N_Y, targets_n // N_Y, shard), BF16),
            vmem((N_Y - 1, targets_n // N_Y, shard), BF16),
            vmem((N_LO * each * SLOT, LANES), F32),
            vmem((N_LO, each, SLOT, LANES), BF16),
            vmem((N_LO - 1, each, SLOT, LANES), BF16),
            vmem((each * SLOT, LANES), F32),
            dma((near,)), dma((near,)), dma((far,)), dma((far,)),
            dma((peers,)), dma((peers,)), dma((peers,)), dma((peers,)),
            dma((N_Y - 1,)), dma((N_Y - 1,)), dma((N_LO - 1,)), dma((N_LO - 1,)), dma,
        ],
        compiler_params=pltpu.CompilerParams(collective_id=0, has_side_effects=True, vmem_limit_bytes=40 << 20),
        name="exchange_operator",
    )(
        orbitals, targets.reshape(1, -1), points.reshape(1, -1), fit,
        jnp.asarray(left), jnp.asarray(lines), jnp.asarray(square),
    )


def solution(mesh):
    in_specs = (P(None, "grid"), P(), P("slab"), P("slab", None))
    out_specs = P("slab", "grid")
    return jax.shard_map(body, mesh=mesh, in_specs=in_specs, out_specs=out_specs, check_vma=False)
```

time: 856 us -> 123 us (0.14)
  waiting for transfers between devices: 489 us -> 0 us
  blocking collectives: 289 us -> 0 us
  Pallas kernels: 0 us -> 117 us
  starting transfers between devices: 25.5 us -> 0 us
  matrix products: 22.6 us -> 0 us
  between operations: 14.3 us -> 0.02 us
    unnamed x2 -> x0, waiting for transfers between devices: 456 us -> none
    psum x1 -> x0, blocking collectives: 245 us -> none  [body(): at_points = lax.psum(point_terms, 'grid').astype(jnp.bfloat16)]
    pallas_call x0 -> x1, Pallas kernels: none -> 117 us  [body(): pl.pallas_call(functools.partial(kernel, occupied, targets_n, group, shar...]
    all_to_all x1 -> x0, blocking collectives: 43.6 us -> none  [body(): lax.all_to_all(potential, 'grid', split_axis=1, concat_axis=0, tiled=True)]
    all_to_all x1 -> x0, waiting for transfers between devices: 33.1 us -> none  [body(): lax.all_to_all(fitted, 'grid', split_axis=0, concat_axis=1, tiled=True)]
    all_to_all x1 -> x0, starting transfers between devices: 25.3 us -> none  [body(): lax.all_to_all(fitted, 'grid', split_axis=0, concat_axis=1, tiled=True)]
    dot_general x27 -> x0, matrix products: 22.6 us -> none  [the longest x18 17 us: apply_axis(): jnp.einsum(pattern, values, matrix, precision=careful, preferred_element_...]
  transfers between devices with their start and end apart: 2 -> 0, of which waited for: 2 -> 0; matrix products, arithmetic and copies ran while one was open for 0% -> 0% of each run, Pallas kernels for 0% -> 0%
where the time goes in v2:
time: 123 us; the launch traced here: 122 us
  Pallas kernels  117 us (95%)
  local copies, waits for them, and re-layouts  5.29 us (4%)
    pallas_call x1, Pallas kernels, body(): pl.pallas_call(functools.partial(kernel, occupied, targets_n, group, shar...  117 us
    unnamed x15, local copies, waits for them, and re-layouts  5.29 us

profile of v2, /device:TPU:6, one launch (start us, length us, event | category | flops | bytes accessed | tf_op | source)
XLA Modules:
  0.0 122.3 jit_solution(17188061699069679533)
XLA Ops:
  0.0 0.0 copy-start.5
  0.0 0.0 copy-start.6
  0.0 0.7 copy-done.5
  0.7 0.0 copy-done.6
  0.7 0.0 copy-start
  0.7 1.0 copy-done
  1.7 0.0 copy-start.1
  1.7 0.8 copy-done.1
  2.5 0.0 copy-start.2
  2.5 0.7 copy-done.2
  3.2 0.0 copy-start.3
  3.2 0.7 copy-done.3
  4.0 0.0 copy-start.4
  4.0 0.7 copy-done.4
  4.7 117.0 %exchange_operator.1 = f32[2,3456]{1,0:T(2,128)S(1)} custom-call(bf16[64,3456]{1,0:T(8,128)(2,1)S(1)} %copy-done, s32[1,64]{1,0:T(1,128)S(1)} %bitcast.2, s32[1,32]{1,0:T(1,128)S(1)} %bitcast.3, f32[32,32]{1,0:T(8,128)S(1)} %copy-done.4, bf16[2,48,144]{2,1,0:T(8,128)(2,1)S(1)} %copy-done.1, bf16[96,128]{1,0:T(8,128)(2,1)S(1)} %copy-done.3, ...), custom_call_target="tpu_custom_call" | custom-call | tf_op jit(solution)/shard_map/exchange_operator/pallas_call | solution.py:334
  121.7 0.6 copy.9
Async XLA Ops:
  0.0 0.7 copy-start.5
  0.0 0.7 copy-start.6
  0.7 1.0 copy-start
  1.7 0.8 copy-start.1
  2.5 0.7 copy-start.2
  3.2 0.7 copy-start.3
  4.0 0.7 copy-start.4

commit v3 on v2

--- a/solution.py
+++ b/solution.py
@@ -17,6 +17,7 @@
 N_GRID = N_X * N_HI * N_CORE
 LANES = 128
 SLOT = 32
+PIECE = 16
 F32, BF16 = jnp.float32, jnp.bfloat16
 
 
@@ -75,22 +76,27 @@
     return jnp.sum(jnp.where(same, row, 0), axis=1, keepdims=True)
 
 
+def row_of(tile):
+    return tile + (tile >= PIECE - 1)
+
+
 def spans(line):
     return range(line * NG // LANES, (line * NG + NG - 1) // LANES + 1)
 
 
 def kernel(
-    occupied, targets_n, group, shard, orb_ref, targets_ref, points_ref, fit_ref, left_ref, lines_ref, square_ref,
-    out_ref, mine, near, part, far, chosen, density, flat, packed, cells, cube, weights, zline,
+    occupied, targets_n, group, shard, orb_hbm, targets_hbm, points_hbm, fit_hbm, left_hbm, lines_hbm, square_hbm,
+    out_ref, orb_ref, targets_ref, points_ref, fit_ref, left_ref, lines_ref, square_ref, mine, near, part, far, chosen, density, flat, packed, cells, cube, weights, zline,
     send_a, recv_a, send_b, recv_b, y_out, y_in, lo_flat, lo_out, lo_in, last,
-    near_s, near_r, far_s, far_r, a_s, a_r, b_s, b_r, y_s, y_r, lo_s, lo_r, local,
+    near_s, near_r, far_s, far_r, a_s, a_r, b_s, b_r, y_s, y_r, lo_s, lo_r, local, fetched,
 ):
     grid, slab = lax.axis_index("grid"), lax.axis_index("slab")
     core, hi, x = lax.rem(grid, N_CORE), lax.rem(grid // N_CORE, N_HI), grid // (N_CORE * N_HI)
     lo, y = slab // N_Y, lax.rem(slab, N_Y)
     tiles = shard // LANES
     rows = tiles // 3
-    wire = tiles + tiles % 2
+    wire = row_of(tiles - 1) + 1
+    pieces = [(0, PIECE, range((PIECE - 1) // 3)), (PIECE, wire, range((PIECE - 1) // 3, rows))]
     each = targets_n // (N_LO * N_Y)
 
     def grid_peer(dx, dh, dc):
@@ -102,7 +108,16 @@
     def lo_peer(d):
         return lax.rem(lo + d, N_LO) * N_Y + y
 
-    offsets = [(dx, dh, dc) for dh in (2, 1, 3, 0) for dx in range(N_X) for dc in range(N_CORE) if dx or dh or dc]
+    offsets = [(dx, dh, dc) for dx in (2, 1, 3, 0) for dc in (1, 0) for dh in (2, 1, 3, 0) if dx or dh or dc]
+    fetches = [
+        pltpu.make_async_copy(source, target, fetched.at[i])
+        for i, (source, target) in enumerate(
+            [
+                (points_hbm, points_ref), (orb_hbm, orb_ref), (targets_hbm, targets_ref), (lines_hbm, lines_ref),
+                (square_hbm, square_ref), (fit_hbm, fit_ref), (left_hbm, left_ref),
+            ]
+        )
+    ]
     barrier = pltpu.get_barrier_semaphore()
     for step in offsets:
         pl.semaphore_signal(barrier, inc=1, device_id={"grid": grid_peer(*step)}, device_id_type=MESH)
@@ -111,6 +126,9 @@
     for d in range(1, N_LO):
         pl.semaphore_signal(barrier, inc=1, device_id={"slab": lo_peer(d)}, device_id_type=MESH)
 
+    for fetch in fetches:
+        fetch.start()
+
     def push(src, dst, send, recv, peer):
         copy = pltpu.make_async_remote_copy(
             src_ref=src, dst_ref=dst, send_sem=send, recv_sem=recv, device_id=peer, device_id_type=MESH
@@ -118,6 +136,11 @@
         copy.start()
         return copy
 
+    flat[...] = jnp.zeros_like(flat)
+    lo_flat[...] = jnp.zeros_like(lo_flat)
+    zline[...] = jnp.zeros_like(zline)
+    for fetch in fetches:
+        fetch.wait()
     offset = column_of(points_ref[...], group) - grid * shard
     for i in range(rows):
         ids = lax.broadcasted_iota(jnp.int32, (group, 384), 1) + i * 384
@@ -138,13 +161,10 @@
     reorder = dot(jnp.where(old == from_old, 1.0, 0.0).astype(BF16), pick).astype(BF16)
     for i in range(rows):
         chosen[:, i * 384 : (i + 1) * 384] = dot(pick, orb_ref[:, i * 384 : (i + 1) * 384]).astype(BF16)
-    zline[...] = jnp.zeros_like(zline)
     for line in range(8):
         at = slice(line * NG, (line + 1) * NG)
         for k in range(2):
             zline[k, at, line * LANES : (line + 1) * LANES] = lines_ref[k * NG : (k + 1) * NG, :]
-    flat[...] = jnp.zeros_like(flat)
-    lo_flat[...] = jnp.zeros_like(lo_flat)
     column, row = square_ref[:NG, :], square_ref[NG : NG + 1, :]
 
     def weigh(m, carry):
@@ -195,32 +215,33 @@
         pair_3 = (rest - pair_2.astype(F32)).astype(BF16)
         fitted = dot(fits, jnp.concatenate([pair_1, pair_2, pair_1, pair_3, pair_2, pair_1], axis=0))
         for t in range(3):
-            flat[pl.ds(3 * i + t, group, stride=SLOT), :] = fitted[:, t * LANES : (t + 1) * LANES]
+            flat[pl.ds(row_of(3 * i + t), group, stride=SLOT), :] = fitted[:, t * LANES : (t + 1) * LANES]
     send_a[...] = flat[...].reshape(N_GRID, SLOT, LANES).astype(BF16)
 
-    def spread(source, target, send, recv):
-        own = pltpu.make_async_copy(source.at[grid], target.at[grid], local)
-        own.start()
+    def spread(source, target, send, recv, first, past):
         copies = []
         for i, step in enumerate(offsets):
             peer = grid_peer(*step)
             copies.append(
                 push(
-                    source.at[peer, pl.ds(0, wire)], target.at[grid, pl.ds(0, wire)], send.at[i], recv.at[i],
-                    {"grid": peer},
+                    source.at[peer, pl.ds(first, past - first)], target.at[grid, pl.ds(first, past - first)],
+                    send.at[i], recv.at[i], {"grid": peer},
                 )
             )
-        own.wait()
-        for copy in copies:
-            copy.wait()
-        flat[...] = target[...].astype(F32).reshape(N_GRID * SLOT, LANES)
-
-    spread(send_a, recv_a, a_s, a_r)
+        return copies
+
+    own = pltpu.make_async_copy(send_a.at[grid], recv_a.at[grid], local)
+    copies = spread(send_a, recv_a, a_s, a_r, 0, wire)
+    own.start()
+    own.wait()
+    for copy in copies:
+        copy.wait()
+    flat[...] = recv_a[...].astype(F32).reshape(N_GRID * SLOT, LANES)
 
     for i in range(rows):
         for t in range(3):
             packed[i * N_GRID : (i + 1) * N_GRID, t * LANES : (t + 1) * LANES] = flat[
-                pl.ds(3 * i + t, N_GRID, stride=SLOT), :
+                pl.ds(row_of(3 * i + t), N_GRID, stride=SLOT), :
             ].astype(BF16)
     for line in range(8):
         at = slice(line * LANES, (line + 1) * LANES)
@@ -281,45 +302,60 @@
             tile[t] = term if tile[t] is None else tile[t] + term
     for i in range(rows):
         for t in range(3):
-            flat[pl.ds(3 * i + t, N_GRID, stride=SLOT), :] = tile[t][i * N_GRID : (i + 1) * N_GRID, :]
+            flat[pl.ds(row_of(3 * i + t), N_GRID, stride=SLOT), :] = tile[t][i * N_GRID : (i + 1) * N_GRID, :]
     send_b[...] = flat[...].reshape(N_GRID, SLOT, LANES).astype(BF16)
 
-    spread(send_b, recv_b, b_s, b_r)
-
-    for i in range(rows):
-        at = slice(i * 384, (i + 1) * 384)
-        got = jnp.concatenate([flat[pl.ds(3 * i + t, group, stride=SLOT), :] for t in range(3)], axis=1)
-        weighted = (got * density[:, at]).astype(BF16)
-        y_out[:, :, at] = dot(ordered, weighted).astype(BF16).reshape(N_Y, targets_n // N_Y, 384)
-    copies = [
-        push(y_out.at[lax.rem(y + d, N_Y)], y_in.at[d - 1], y_s.at[d - 1], y_r.at[d - 1], {"slab": y_peer(d)})
-        for d in range(1, N_Y)
-    ]
-    for copy in copies:
-        copy.wait()
-    for i in range(rows):
-        at = slice(i * 384, (i + 1) * 384)
-        total = y_out[y, :, at].astype(F32)
-        for d in range(N_Y - 1):
-            total = total + y_in[d, :, at].astype(F32)
-        for t in range(3):
-            lo_flat[pl.ds(3 * i + t, N_LO * each, stride=SLOT), :] = total[:, t * LANES : (t + 1) * LANES]
-    lo_out[...] = lo_flat[...].reshape(N_LO, each, SLOT, LANES).astype(BF16)
-    copies = [
-        push(
-            lo_out.at[lax.rem(lo + d, N_LO), :, pl.ds(0, wire)], lo_in.at[d - 1, :, pl.ds(0, wire)],
-            lo_s.at[d - 1], lo_r.at[d - 1], {"slab": lo_peer(d)},
-        )
-        for d in range(1, N_LO)
-    ]
-    for copy in copies:
+    own = pltpu.make_async_copy(send_b.at[grid], recv_b.at[grid], local)
+    spreads = [spread(send_b, recv_b, b_s.at[p], b_r.at[p], first, past) for p, (first, past, _) in enumerate(pieces)]
+    own.start()
+    own.wait()
+    sums = []
+    for p, (first, past, span) in enumerate(pieces):
+        for copy in spreads[p]:
+            copy.wait_recv()
+        flat[: N_GRID * PIECE, :] = recv_b[:, first : first + PIECE, :].astype(F32).reshape(N_GRID * PIECE, LANES)
+        for i in span:
+            at = slice(i * 384, (i + 1) * 384)
+            got = [flat[pl.ds(row_of(3 * i + t) - first, group, stride=PIECE), :] for t in range(3)]
+            weighted = (jnp.concatenate(got, axis=1) * density[:, at]).astype(BF16)
+            y_out[:, :, at] = dot(ordered, weighted).astype(BF16).reshape(N_Y, targets_n // N_Y, 384)
+        lanes = pl.ds(span[0] * 384, len(span) * 384)
+        copies = [
+            push(
+                y_out.at[lax.rem(y + d, N_Y), :, lanes], y_in.at[d - 1, :, lanes],
+                y_s.at[p, d - 1], y_r.at[p, d - 1], {"slab": y_peer(d)},
+            )
+            for d in range(1, N_Y)
+        ]
+        for copy in copies:
+            copy.wait()
+        for i in span:
+            at = slice(i * 384, (i + 1) * 384)
+            total = y_out[y, :, at].astype(F32)
+            for d in range(N_Y - 1):
+                total = total + y_in[d, :, at].astype(F32)
+            for t in range(3):
+                lo_flat[pl.ds(row_of(3 * i + t), N_LO * each, stride=SLOT), :] = total[:, t * LANES : (t + 1) * LANES]
+        half = lo_flat[...].reshape(N_LO * each, SLOT, LANES)[:, first : first + PIECE, :].astype(BF16)
+        lo_out[:, :, first : first + PIECE, :] = half.reshape(N_LO, each, PIECE, LANES)
+        sums += [
+            push(
+                lo_out.at[lax.rem(lo + d, N_LO), :, pl.ds(first, past - first)],
+                lo_in.at[d - 1, :, pl.ds(first, past - first)],
+                lo_s.at[p, d - 1], lo_r.at[p, d - 1], {"slab": lo_peer(d)},
+            )
+            for d in range(1, N_LO)
+        ]
+    for copy in spreads[0] + spreads[1]:
+        copy.wait_send()
+    for copy in sums:
         copy.wait()
     total = lo_out[lo].astype(F32)
     for d in range(N_LO - 1):
         total = total + lo_in[d].astype(F32)
     last[...] = (total * (-1.0 / math.sqrt(group * N_LO * N_Y))).reshape(each * SLOT, LANES)
     for c in range(tiles):
-        out_ref[:, c * LANES : (c + 1) * LANES] = last[pl.ds(c, each, stride=SLOT), :]
+        out_ref[:, c * LANES : (c + 1) * LANES] = last[pl.ds(row_of(c), each, stride=SLOT), :]
 
 
 def body(orbitals, targets, points, fit):
@@ -334,9 +370,16 @@
     return pl.pallas_call(
         functools.partial(kernel, occupied, targets_n, group, shard),
         out_shape=jax.ShapeDtypeStruct((each, shard), F32),
-        in_specs=[pl.BlockSpec(memory_space=pltpu.VMEM)] * 7,
+        in_specs=[pl.BlockSpec(memory_space=pl.ANY)] * 7,
         out_specs=pl.BlockSpec(memory_space=pltpu.VMEM),
         scratch_shapes=[
+            vmem(orbitals.shape, BF16),
+            vmem((1, targets_n), jnp.int32),
+            vmem((1, group), jnp.int32),
+            vmem(fit.shape, F32),
+            vmem(left.shape, BF16),
+            vmem(lines.shape, BF16),
+            vmem(square.shape, F32),
             vmem((group, occupied), BF16),
             vmem((near, group, occupied), BF16),
             vmem((group, occupied), BF16),
@@ -360,10 +403,10 @@
             vmem((N_LO - 1, each, SLOT, LANES), BF16),
             vmem((each * SLOT, LANES), F32),
             dma((near,)), dma((near,)), dma((far,)), dma((far,)),
-            dma((peers,)), dma((peers,)), dma((peers,)), dma((peers,)),
-            dma((N_Y - 1,)), dma((N_Y - 1,)), dma((N_LO - 1,)), dma((N_LO - 1,)), dma,
+            dma((peers,)), dma((peers,)), dma((2, peers)), dma((2, peers)),
+            dma((2, N_Y - 1)), dma((2, N_Y - 1)), dma((2, N_LO - 1)), dma((2, N_LO - 1)), dma, dma((7,)),
         ],
-        compiler_params=pltpu.CompilerParams(collective_id=0, has_side_effects=True, vmem_limit_bytes=40 << 20),
+        compiler_params=pltpu.CompilerParams(collective_id=0, has_side_effects=True, vmem_limit_bytes=60 * 1024 * 1024),
         name="exchange_operator",
     )(
         orbitals, targets.reshape(1, -1), points.reshape(1, -1), fit,

time: 123 us -> 119 us (0.967)
  local copies, waits for them, and re-layouts: 5.29 us -> 1.36 us
    unnamed x15 -> x1, local copies, waits for them, and re-layouts: 5.29 us -> 1.36 us
where the time goes in v3:
time: 119 us; the launch traced here: 118 us
  Pallas kernels  117 us (98%)
  local copies, waits for them, and re-layouts  1.36 us (1%)
    pallas_call x1, Pallas kernels, body(): pl.pallas_call(functools.partial(kernel, occupied, targets_n, group, shar...  117 us

profile of v3, /device:TPU:6, one launch (start us, length us, event | category | flops | bytes accessed | tf_op | source)
XLA Modules:
  0.0 118.2 jit_solution(13650066809686290330)
XLA Ops:
  0.0 116.9 %exchange_operator.1 = f32[2,3456]{1,0:T(2,128)} custom-call(bf16[64,3456]{1,0:T(8,128)(2,1)} %orb_hbm.1, s32[1,64]{1,0:T(1,128)} %bitcast.2, s32[1,32]{1,0:T(1,128)} %bitcast.3, f32[32,32]{1,0:T(8,128)} %fit_hbm.1, bf16[2,48,144]{2,1,0:T(8,128)(2,1)} %constant.6.clone.left_hbm, bf16[96,128]{1,0:T(8,128)(2,1)} %constant.7.clone.lines_hbm, ...), custom_call_target="tpu_custom_call" | custom-call | tf_op jit(solution)/shard_map/exchange_operator/pallas_call | solution.py:370
  116.9 1.4 %copy.9 = f32[2,3456]{1,0:T(2,128)} copy(f32[2,3456]{1,0:T(2,128)} %exchange_operator.1) | data formatting | bytes 55296

commit v4 on v3

--- a/solution.py
+++ b/solution.py
@@ -108,7 +108,7 @@
     def lo_peer(d):
         return lax.rem(lo + d, N_LO) * N_Y + y
 
-    offsets = [(dx, dh, dc) for dx in (2, 1, 3, 0) for dc in (1, 0) for dh in (2, 1, 3, 0) if dx or dh or dc]
+    offsets = [(dx, dh, dc) for hs in ((2,), (1, 3), (0,)) for dx in (2, 1, 3, 0) for dc in (1, 0) for dh in hs if dx or dh or dc]
     fetches = [
         pltpu.make_async_copy(source, target, fetched.at[i])
         for i, (source, target) in enumerate(
@@ -256,32 +256,32 @@
 
     many = 8
 
+    def pairs_of(values):
+        return [jnp.concatenate([stack(a), stack(b)], axis=1) for a, b in zip(values[::2], values[1::2])]
+
+    def apart(values):
+        return [v[:, k * LANES : (k + 1) * LANES] for v in values for k in range(2)]
+
     def along_y(which):
         def one(step, carry):
-            for u in range(0, many, 2):
-                first = pl.ds(pl.multiple_of((step * many + u) * NG, NG), NG)
-                second = pl.ds(pl.multiple_of((step * many + u + 1) * NG, NG), NG)
-                both = jnp.concatenate([stack(cube[first, :]), stack(cube[second, :])], axis=1)
-                got = dot(left_ref[which], both)
-                cube[first, :] = got[:, :LANES]
-                cube[second, :] = got[:, LANES:]
+            at = [pl.ds(pl.multiple_of((step * many + u) * NG, NG), NG) for u in range(many)]
+            left = left_ref[which]
+            got = apart([dot(left, both) for both in pairs_of([cube[a, :] for a in at])])
+            for a, value in zip(at, got):
+                cube[a, :] = value
             return carry
 
         lax.fori_loop(0, NG // many, one, 0)
 
     def along_x(step, carry):
-        for u in range(0, many, 2):
-            first, second = step * many + u, step * many + u + 1
-            at = [pl.ds(m, NG, stride=NG) for m in (first, second)]
-            both = jnp.concatenate([stack(cube[at[0], :]), stack(cube[at[1], :])], axis=1)
-            got = dot(left_ref[0], both)
-            got = [
-                got[:, k * LANES : (k + 1) * LANES] * weights[pl.ds(pl.multiple_of(m * NG, NG), NG), :]
-                for k, m in enumerate((first, second))
-            ]
-            got = dot(left_ref[1], jnp.concatenate([stack(got[0]), stack(got[1])], axis=1))
-            cube[at[0], :] = got[:, :LANES]
-            cube[at[1], :] = got[:, LANES:]
+        at = [pl.ds(step * many + u, NG, stride=NG) for u in range(many)]
+        scale = [pl.ds(pl.multiple_of((step * many + u) * NG, NG), NG) for u in range(many)]
+        left, back = left_ref[0], left_ref[1]
+        got = apart([dot(left, both) for both in pairs_of([cube[a, :] for a in at])])
+        got = [value * weights[m, :] for value, m in zip(got, scale)]
+        got = apart([dot(back, both) for both in pairs_of(got)])
+        for a, value in zip(at, got):
+            cube[a, :] = value
         return carry
 
     along_y(0)

time: 119 us -> 119 us (level)
  no operation moved by 1% of the time
where the time goes in v4:
time: 119 us
  Pallas kernels  117 us (98%)
  local copies, waits for them, and re-layouts  1.36 us (1%)
    pallas_call x1, Pallas kernels, body(): pl.pallas_call(functools.partial(kernel, occupied, targets_n, group, shar...  117 us

profile of v4, /device:TPU:6, one launch (start us, length us, event | category | flops | bytes accessed | tf_op | source)
XLA Modules:
  0.0 118.7 jit_solution(7618236988834512334)
XLA Ops:
  0.0 117.4 %exchange_operator.1 = f32[2,3456]{1,0:T(2,128)} custom-call(bf16[64,3456]{1,0:T(8,128)(2,1)} %orb_hbm.1, s32[1,64]{1,0:T(1,128)} %bitcast.2, s32[1,32]{1,0:T(1,128)} %bitcast.3, f32[32,32]{1,0:T(8,128)} %fit_hbm.1, bf16[2,48,144]{2,1,0:T(8,128)(2,1)} %constant.6.clone.left_hbm, bf16[96,128]{1,0:T(8,128)(2,1)} %constant.7.clone.lines_hbm, ...), custom_call_target="tpu_custom_call" | custom-call | tf_op jit(solution)/shard_map/exchange_operator/pallas_call | solution.py:370
  117.4 1.4 %copy.9 = f32[2,3456]{1,0:T(2,128)} copy(f32[2,3456]{1,0:T(2,128)} %exchange_operator.1) | data formatting | bytes 55296

commit v5 on v4

--- a/solution.py
+++ b/solution.py
@@ -86,9 +86,9 @@
 
 def kernel(
     occupied, targets_n, group, shard, orb_hbm, targets_hbm, points_hbm, fit_hbm, left_hbm, lines_hbm, square_hbm,
-    out_ref, orb_ref, targets_ref, points_ref, fit_ref, left_ref, lines_ref, square_ref, mine, near, part, far, chosen, density, flat, packed, cells, cube, weights, zline,
+    out_ref, orb_ref, targets_ref, points_ref, fit_ref, left_ref, lines_ref, square_ref, mine, near, part, far, home_at, task_at, task_fit, task_orb, density, flat, packed, cells, cube, weights, zline,
     send_a, recv_a, send_b, recv_b, y_out, y_in, lo_flat, lo_out, lo_in, last,
-    near_s, near_r, far_s, far_r, a_s, a_r, b_s, b_r, y_s, y_r, lo_s, lo_r, local, fetched,
+    near_s, near_r, far_s, far_r, orb_s, orb_r, all_s, all_r, at_s, at_r, fit_s, fit_r, a_s, a_r, b_s, b_r, y_s, y_r, lo_s, lo_r, local, fetched,
 ):
     grid, slab = lax.axis_index("grid"), lax.axis_index("slab")
     core, hi, x = lax.rem(grid, N_CORE), lax.rem(grid // N_CORE, N_HI), grid // (N_CORE * N_HI)
@@ -99,16 +99,45 @@
     pieces = [(0, PIECE, range((PIECE - 1) // 3)), (PIECE, wire, range((PIECE - 1) // 3, rows))]
     each = targets_n // (N_LO * N_Y)
 
+    half, place = lo // N_HI, lax.rem(lo, N_HI)
+    at_home = place == hi
+    quarter = occupied // N_Y
+
     def grid_peer(dx, dh, dc):
         return (lax.rem(x + dx, N_X) * N_HI + lax.rem(hi + dh, N_HI)) * N_CORE + lax.rem(core + dc, N_CORE)
 
+    def place_slab(where):
+        return (half * N_HI + where) * N_Y + y
+
+    def task_peer(dx, dp, dc):
+        return {"grid": grid_peer(dx, 0, dc), "slab": place_slab(lax.rem(place + dp, N_HI))}
+
+    def vector_of(dx, dp, dc):
+        return (lax.rem(x + dx, N_X) * N_HI + lax.rem(place + dp, N_HI)) * N_CORE + lax.rem(core + dc, N_CORE)
+
+    vector = vector_of(0, 0, 0)
+
+    def block_of(dx, dp, dc):
+        return (lax.rem(x + dx, N_X) * N_HI + lax.rem(place + dp + hi, N_HI)) * N_CORE + lax.rem(core + dc, N_CORE)
+
+    block = block_of(0, 0, 0)
+    away = place != 0
+
+    def cells_peer(d):
+        return {"grid": grid_peer(0, place, 0), "slab": lax.rem(lo + d, N_LO) * N_Y + y}
+
+    def source_peer(dh, da):
+        where = lax.rem(half + da, N_LO // N_HI) * N_HI + lax.rem(N_HI + N_HI - dh, N_HI)
+        return {"grid": grid_peer(0, dh, 0), "slab": where * N_Y + y}
+
     def y_peer(d):
         return lo * N_Y + lax.rem(y + d, N_Y)
 
-    def lo_peer(d):
-        return lax.rem(lo + d, N_LO) * N_Y + y
-
-    offsets = [(dx, dh, dc) for hs in ((2,), (1, 3), (0,)) for dx in (2, 1, 3, 0) for dc in (1, 0) for dh in hs if dx or dh or dc]
+    def steps(order):
+        return [(dx, d, dc) for ds in order for dx in (2, 1, 3, 0) for dc in (1, 0) for d in ds]
+
+    tasks = [step for step in steps(((2,), (1, 3), (0,))) if any(step)]
+    sources = [(dh, da) for dh in range(N_HI) for da in range(N_LO // N_HI)]
     fetches = [
         pltpu.make_async_copy(source, target, fetched.at[i])
         for i, (source, target) in enumerate(
@@ -119,13 +148,20 @@
         )
     ]
     barrier = pltpu.get_barrier_semaphore()
-    for step in offsets:
-        pl.semaphore_signal(barrier, inc=1, device_id={"grid": grid_peer(*step)}, device_id_type=MESH)
+
+    def hello(peer):
+        pl.semaphore_signal(barrier, inc=1, device_id=peer, device_id_type=MESH)
+
+    for d in range(1, N_HI):
+        hello({"grid": grid_peer(0, d, 0)})
+    for step in sources:
+        if any(step):
+            hello(source_peer(*step))
+    pl.when(away)(lambda: hello(source_peer(0, 0)))
+    for step in tasks:
+        hello(task_peer(*step))
     for d in range(1, N_Y):
         pl.semaphore_signal(barrier, inc=1, device_id={"slab": y_peer(d)}, device_id_type=MESH)
-    for d in range(1, N_LO):
-        pl.semaphore_signal(barrier, inc=1, device_id={"slab": lo_peer(d)}, device_id_type=MESH)
-
     for fetch in fetches:
         fetch.start()
 
@@ -159,8 +195,6 @@
     old = lax.broadcasted_iota(jnp.int32, (targets_n, targets_n), 1)
     from_old = ((new // each) % N_LO) * (N_Y * each) + (new // (each * N_LO)) * each + new % each
     reorder = dot(jnp.where(old == from_old, 1.0, 0.0).astype(BF16), pick).astype(BF16)
-    for i in range(rows):
-        chosen[:, i * 384 : (i + 1) * 384] = dot(pick, orb_ref[:, i * 384 : (i + 1) * 384]).astype(BF16)
     for line in range(8):
         at = slice(line * NG, (line + 1) * NG)
         for k in range(2):
@@ -173,13 +207,17 @@
         return carry
 
     lax.fori_loop(0, NG, weigh, 0)
-    fit = fit_ref[...]
-    fit_1 = fit.astype(BF16)
-    fit_2 = (fit - fit_1.astype(F32)).astype(BF16)
-    fit_3 = (fit - fit_1.astype(F32) - fit_2.astype(F32)).astype(BF16)
-    fits = jnp.concatenate([fit_1, fit_1, fit_2, fit_1, fit_2, fit_3], axis=1)
-
-    pl.semaphore_wait(barrier, len(offsets) + N_Y - 1 + N_LO - 1)
+    greetings = N_HI - 1 + len(tasks) + N_LO - 1 + N_Y - 1
+    pl.semaphore_wait(barrier, greetings + jnp.where(away, 1, 0))
+
+    own_rows = pl.ds(pl.multiple_of(y * quarter, quarter), quarter)
+    fetch_orb = pltpu.make_async_remote_copy(
+        src_ref=orb_ref.at[own_rows], dst_ref=task_orb.at[own_rows], send_sem=orb_s, recv_sem=orb_r,
+        device_id={"grid": grid_peer(0, N_HI - place, 0)}, device_id_type=MESH,
+    )
+    keep_orb = pltpu.make_async_copy(orb_ref.at[own_rows], task_orb.at[own_rows], orb_r)
+    pl.when(away)(fetch_orb.start)
+    pl.when(jnp.logical_not(away))(keep_orb.start)
 
     near_steps = [(dx, 0, dc) for dx in range(N_X) for dc in range(N_CORE) if dx or dc]
     copies = [
@@ -201,14 +239,59 @@
     for i in range(N_HI - 1):
         total = total + far[i].astype(F32)
     at_points = total.astype(BF16)
-
-    target_points = dot(at_points, choose).astype(BF16)
-    ordered = dot_nt(reorder, at_points).astype(BF16)
+    home_at[...] = at_points
+
+    def hand(source, target, send, recv):
+        return [
+            pltpu.make_async_remote_copy(
+                src_ref=source, dst_ref=target, send_sem=send.at[d - 1], recv_sem=recv,
+                device_id=task_peer(0, d, 0), device_id_type=MESH,
+            )
+            for d in range(1, N_HI)
+        ]
+
+    hands = hand(home_at, task_at, at_s, at_r) + hand(fit_ref, task_fit, fit_s, fit_r)
+
+    @pl.when(at_home)
+    def _():
+        for copy in hands:
+            copy.start()
+        task_at[...] = home_at[...]
+        task_fit[...] = fit_ref[...]
+
+    fetch_orb.wait_recv()
+    copies = [
+        push(task_orb.at[own_rows], task_orb.at[own_rows], all_s.at[d - 1], all_r.at[d - 1], {"slab": y_peer(d)})
+        for d in range(1, N_Y)
+    ]
+    @pl.when(jnp.logical_not(at_home))
+    def _():
+        hands[0].wait_recv()
+        hands[-1].wait_recv()
+
+    at_task = task_at[...]
+    ordered = dot_nt(reorder, at_task).astype(BF16)
+    fit = task_fit[...]
+    fit_1 = fit.astype(BF16)
+    fit_2 = (fit - fit_1.astype(F32)).astype(BF16)
+    fit_3 = (fit - fit_1.astype(F32) - fit_2.astype(F32)).astype(BF16)
+    fits = jnp.concatenate([fit_1, fit_1, fit_2, fit_1, fit_2, fit_3], axis=1)
+    target_points = dot(at_task, choose).astype(BF16)
+    for d, copy in enumerate(copies):
+        copy.wait_send()
+    for d in range(1, N_Y):
+        their_rows = pl.ds(pl.multiple_of(lax.rem(y + N_Y - d, N_Y) * quarter, quarter), quarter)
+        pltpu.make_async_remote_copy(
+            src_ref=task_orb.at[their_rows], dst_ref=task_orb.at[their_rows], send_sem=all_s.at[d - 1],
+            recv_sem=all_r.at[d - 1], device_id={"slab": y_peer(d)}, device_id_type=MESH,
+        ).wait_recv()
     for i in range(rows):
         at = slice(i * 384, (i + 1) * 384)
-        dense = dot(at_points, orb_ref[:, at]) * (1.0 / math.sqrt(occupied))
+        orb = task_orb[:, at]
+        dense = dot(at_task, orb) * (1.0 / math.sqrt(occupied))
         density[:, at] = dense
-        pair = dense * (dot(target_points, chosen[:, at]) * (1.0 / math.sqrt(targets_n)))
+        chosen = dot(pick, orb).astype(BF16)
+        pair = dense * (dot(target_points, chosen) * (1.0 / math.sqrt(targets_n)))
         pair_1 = pair.astype(BF16)
         rest = pair - pair_1.astype(F32)
         pair_2 = rest.astype(BF16)
@@ -218,24 +301,28 @@
             flat[pl.ds(row_of(3 * i + t), group, stride=SLOT), :] = fitted[:, t * LANES : (t + 1) * LANES]
     send_a[...] = flat[...].reshape(N_GRID, SLOT, LANES).astype(BF16)
 
-    def spread(source, target, send, recv, first, past):
-        copies = []
-        for i, step in enumerate(offsets):
-            peer = grid_peer(*step)
-            copies.append(
-                push(
-                    source.at[peer, pl.ds(first, past - first)], target.at[grid, pl.ds(first, past - first)],
-                    send.at[i], recv.at[i], {"grid": peer},
-                )
-            )
-        return copies
-
-    own = pltpu.make_async_copy(send_a.at[grid], recv_a.at[grid], local)
-    copies = spread(send_a, recv_a, a_s, a_r, 0, wire)
+    copies = [
+        push(
+            send_a.at[vector_of(*step), pl.ds(0, wire)], recv_a.at[block, pl.ds(0, wire)],
+            a_s.at[i], a_r.at[i], task_peer(*step),
+        )
+        for i, step in enumerate(tasks)
+    ]
+    own = pltpu.make_async_copy(send_a.at[vector], recv_a.at[block], local)
     own.start()
     own.wait()
     for copy in copies:
         copy.wait()
+
+    @pl.when(away)
+    def _():
+        fetch_orb.wait_send()
+
+    @pl.when(at_home)
+    def _():
+        for copy in hands:
+            copy.wait_send()
+
     flat[...] = recv_a[...].astype(F32).reshape(N_GRID * SLOT, LANES)
 
     for i in range(rows):
@@ -305,11 +392,21 @@
             flat[pl.ds(row_of(3 * i + t), N_GRID, stride=SLOT), :] = tile[t][i * N_GRID : (i + 1) * N_GRID, :]
     send_b[...] = flat[...].reshape(N_GRID, SLOT, LANES).astype(BF16)
 
-    own = pltpu.make_async_copy(send_b.at[grid], recv_b.at[grid], local)
-    spreads = [spread(send_b, recv_b, b_s.at[p], b_r.at[p], first, past) for p, (first, past, _) in enumerate(pieces)]
+    spreads = [
+        [
+            push(
+                send_b.at[block_of(*step), pl.ds(first, past - first)],
+                recv_b.at[vector, pl.ds(first, past - first)], b_s.at[p, i], b_r.at[p, i], task_peer(*step),
+            )
+            for i, step in enumerate(tasks)
+        ]
+        for p, (first, past, _) in enumerate(pieces)
+    ]
+    own = pltpu.make_async_copy(send_b.at[block], recv_b.at[vector], local)
     own.start()
     own.wait()
     sums = []
+    sender = hi * (N_LO // N_HI) + half
     for p, (first, past, span) in enumerate(pieces):
         for copy in spreads[p]:
             copy.wait_recv()
@@ -336,23 +433,37 @@
                 total = total + y_in[d, :, at].astype(F32)
             for t in range(3):
                 lo_flat[pl.ds(row_of(3 * i + t), N_LO * each, stride=SLOT), :] = total[:, t * LANES : (t + 1) * LANES]
-        half = lo_flat[...].reshape(N_LO * each, SLOT, LANES)[:, first : first + PIECE, :].astype(BF16)
-        lo_out[:, :, first : first + PIECE, :] = half.reshape(N_LO, each, PIECE, LANES)
-        sums += [
-            push(
-                lo_out.at[lax.rem(lo + d, N_LO), :, pl.ds(first, past - first)],
-                lo_in.at[d - 1, :, pl.ds(first, past - first)],
-                lo_s.at[p, d - 1], lo_r.at[p, d - 1], {"slab": lo_peer(d)},
-            )
-            for d in range(1, N_LO)
-        ]
+        piece = lo_flat[...].reshape(N_LO * each, SLOT, LANES)[:, first : first + PIECE, :].astype(BF16)
+        lo_out[:, :, first : first + PIECE, :] = piece.reshape(N_LO, each, PIECE, LANES)
+        span_rows = pl.ds(first, past - first)
+        sums.append(
+            [
+                pltpu.make_async_remote_copy(
+                    src_ref=lo_out.at[lax.rem(lo + d, N_LO), :, span_rows], dst_ref=lo_in.at[sender, :, span_rows],
+                    send_sem=lo_s.at[p, d], recv_sem=lo_r.at[p, sender], device_id=cells_peer(d), device_id_type=MESH,
+                )
+                for d in range(N_LO)
+            ]
+        )
+        kept = pltpu.make_async_copy(lo_out.at[lo, :, span_rows], lo_in.at[sender, :, span_rows], lo_r.at[p, sender])
+        pl.when(away)(sums[p][0].start)
+        pl.when(jnp.logical_not(away))(kept.start)
+        for copy in sums[p][1:]:
+            copy.start()
     for copy in spreads[0] + spreads[1]:
         copy.wait_send()
-    for copy in sums:
-        copy.wait()
-    total = lo_out[lo].astype(F32)
-    for d in range(N_LO - 1):
-        total = total + lo_in[d].astype(F32)
+    for p, (first, past, _) in enumerate(pieces):
+        pl.when(away)(sums[p][0].wait_send)
+        for copy in sums[p][1:]:
+            copy.wait_send()
+        for k in range(N_LO):
+            pltpu.make_async_remote_copy(
+                src_ref=lo_out.at[k, :, pl.ds(first, past - first)], dst_ref=lo_in.at[k, :, pl.ds(first, past - first)],
+                send_sem=lo_s.at[p, k], recv_sem=lo_r.at[p, k], device_id=cells_peer(1), device_id_type=MESH,
+            ).wait_recv()
+    total = lo_in[0].astype(F32)
+    for k in range(1, N_LO):
+        total = total + lo_in[k].astype(F32)
     last[...] = (total * (-1.0 / math.sqrt(group * N_LO * N_Y))).reshape(each * SLOT, LANES)
     for c in range(tiles):
         out_ref[:, c * LANES : (c + 1) * LANES] = last[pl.ds(row_of(c), each, stride=SLOT), :]
@@ -384,7 +495,10 @@
             vmem((near, group, occupied), BF16),
             vmem((group, occupied), BF16),
             vmem((far, group, occupied), BF16),
-            vmem((targets_n, shard), BF16),
+            vmem((group, occupied), BF16),
+            vmem((group, occupied), BF16),
+            vmem(fit.shape, F32),
+            vmem(orbitals.shape, BF16),
             vmem((group, shard), F32),
             vmem((N_GRID * SLOT, LANES), F32),
             vmem((N_GRID * shard // 384, 384), BF16),
@@ -400,11 +514,12 @@
             vmem((N_Y - 1, targets_n // N_Y, shard), BF16),
             vmem((N_LO * each * SLOT, LANES), F32),
             vmem((N_LO, each, SLOT, LANES), BF16),
-            vmem((N_LO - 1, each, SLOT, LANES), BF16),
+            vmem((N_LO, each, SLOT, LANES), BF16),
             vmem((each * SLOT, LANES), F32),
             dma((near,)), dma((near,)), dma((far,)), dma((far,)),
+            dma, dma, dma((N_Y - 1,)), dma((N_Y - 1,)), dma((far,)), dma, dma((far,)), dma,
             dma((peers,)), dma((peers,)), dma((2, peers)), dma((2, peers)),
-            dma((2, N_Y - 1)), dma((2, N_Y - 1)), dma((2, N_LO - 1)), dma((2, N_LO - 1)), dma, dma((7,)),
+            dma((2, N_Y - 1)), dma((2, N_Y - 1)), dma((2, N_LO)), dma((2, N_LO)), dma, dma((7,)),
         ],
         compiler_params=pltpu.CompilerParams(collective_id=0, has_side_effects=True, vmem_limit_bytes=60 * 1024 * 1024),
         name="exchange_operator",

time: 119 us -> 111 us (0.933); the launches traced: 119 us -> 110 us
  Pallas kernels: 117 us -> 108 us
    pallas_call x1, Pallas kernels: 117 us -> 108 us  [body(): pl.pallas_call(functools.partial(kernel, occupied, targets_n, group, shar...]
where the time goes in v5:
time: 111 us; the launch traced here: 110 us
  Pallas kernels  108 us (97%)
  local copies, waits for them, and re-layouts  1.36 us (1%)
    pallas_call x1, Pallas kernels, body(): pl.pallas_call(functools.partial(kernel, occupied, targets_n, group, shar...  108 us

profile of v5, /device:TPU:6, one launch (start us, length us, event | category | flops | bytes accessed | tf_op | source)
XLA Modules:
  0.0 109.5 jit_solution(1981409546410929801)
XLA Ops:
  0.0 108.1 %exchange_operator.1 = f32[2,3456]{1,0:T(2,128)} custom-call(bf16[64,3456]{1,0:T(8,128)(2,1)} %orb_hbm.1, s32[1,64]{1,0:T(1,128)} %bitcast.2, s32[1,32]{1,0:T(1,128)} %bitcast.3, f32[32,32]{1,0:T(8,128)} %fit_hbm.1, bf16[2,48,144]{2,1,0:T(8,128)(2,1)} %constant.6.clone.left_hbm, bf16[96,128]{1,0:T(8,128)(2,1)} %constant.7.clone.lines_hbm, ...), custom_call_target="tpu_custom_call" | custom-call | tf_op jit(solution)/shard_map/exchange_operator/pallas_call | solution.py:481
  108.2 1.4 %copy.9 = f32[2,3456]{1,0:T(2,128)} copy(f32[2,3456]{1,0:T(2,128)} %exchange_operator.1) | data formatting | bytes 55296

commit v6 on v5

--- a/solution.py
+++ b/solution.py
@@ -211,13 +211,29 @@
     pl.semaphore_wait(barrier, greetings + jnp.where(away, 1, 0))
 
     own_rows = pl.ds(pl.multiple_of(y * quarter, quarter), quarter)
-    fetch_orb = pltpu.make_async_remote_copy(
-        src_ref=orb_ref.at[own_rows], dst_ref=task_orb.at[own_rows], send_sem=orb_s, recv_sem=orb_r,
-        device_id={"grid": grid_peer(0, N_HI - place, 0)}, device_id_type=MESH,
-    )
-    keep_orb = pltpu.make_async_copy(orb_ref.at[own_rows], task_orb.at[own_rows], orb_r)
-    pl.when(away)(fetch_orb.start)
-    pl.when(jnp.logical_not(away))(keep_orb.start)
+    lane_pieces = [pl.ds(span[0] * 384, len(span) * 384) for _, _, span in pieces]
+    fetch_orb = [
+        pltpu.make_async_remote_copy(
+            src_ref=orb_ref.at[own_rows, lanes], dst_ref=task_orb.at[own_rows, lanes],
+            send_sem=orb_s.at[p], recv_sem=orb_r.at[p],
+            device_id={"grid": grid_peer(0, N_HI - place, 0)}, device_id_type=MESH,
+        )
+        for p, lanes in enumerate(lane_pieces)
+    ]
+    keep_orb = [
+        pltpu.make_async_copy(orb_ref.at[own_rows, lanes], task_orb.at[own_rows, lanes], orb_r.at[p])
+        for p, lanes in enumerate(lane_pieces)
+    ]
+
+    @pl.when(away)
+    def _():
+        for copy in fetch_orb:
+            copy.start()
+
+    @pl.when(jnp.logical_not(away))
+    def _():
+        for copy in keep_orb:
+            copy.start()
 
     near_steps = [(dx, 0, dc) for dx in range(N_X) for dc in range(N_CORE) if dx or dc]
     copies = [
@@ -259,11 +275,17 @@
         task_at[...] = home_at[...]
         task_fit[...] = fit_ref[...]
 
-    fetch_orb.wait_recv()
-    copies = [
-        push(task_orb.at[own_rows], task_orb.at[own_rows], all_s.at[d - 1], all_r.at[d - 1], {"slab": y_peer(d)})
-        for d in range(1, N_Y)
-    ]
+    copies = []
+    for p, lanes in enumerate(lane_pieces):
+        fetch_orb[p].wait_recv()
+        copies += [
+            push(
+                task_orb.at[own_rows, lanes], task_orb.at[own_rows, lanes],
+                all_s.at[p, d - 1], all_r.at[p, d - 1], {"slab": y_peer(d)},
+            )
+            for d in range(1, N_Y)
+        ]
+
     @pl.when(jnp.logical_not(at_home))
     def _():
         hands[0].wait_recv()
@@ -277,59 +299,71 @@
     fit_3 = (fit - fit_1.astype(F32) - fit_2.astype(F32)).astype(BF16)
     fits = jnp.concatenate([fit_1, fit_1, fit_2, fit_1, fit_2, fit_3], axis=1)
     target_points = dot(at_task, choose).astype(BF16)
-    for d, copy in enumerate(copies):
+    for copy in copies:
         copy.wait_send()
-    for d in range(1, N_Y):
-        their_rows = pl.ds(pl.multiple_of(lax.rem(y + N_Y - d, N_Y) * quarter, quarter), quarter)
-        pltpu.make_async_remote_copy(
-            src_ref=task_orb.at[their_rows], dst_ref=task_orb.at[their_rows], send_sem=all_s.at[d - 1],
-            recv_sem=all_r.at[d - 1], device_id={"slab": y_peer(d)}, device_id_type=MESH,
-        ).wait_recv()
-    for i in range(rows):
-        at = slice(i * 384, (i + 1) * 384)
-        orb = task_orb[:, at]
-        dense = dot(at_task, orb) * (1.0 / math.sqrt(occupied))
-        density[:, at] = dense
-        chosen = dot(pick, orb).astype(BF16)
-        pair = dense * (dot(target_points, chosen) * (1.0 / math.sqrt(targets_n)))
-        pair_1 = pair.astype(BF16)
-        rest = pair - pair_1.astype(F32)
-        pair_2 = rest.astype(BF16)
-        pair_3 = (rest - pair_2.astype(F32)).astype(BF16)
-        fitted = dot(fits, jnp.concatenate([pair_1, pair_2, pair_1, pair_3, pair_2, pair_1], axis=0))
-        for t in range(3):
-            flat[pl.ds(row_of(3 * i + t), group, stride=SLOT), :] = fitted[:, t * LANES : (t + 1) * LANES]
-    send_a[...] = flat[...].reshape(N_GRID, SLOT, LANES).astype(BF16)
-
-    copies = [
-        push(
-            send_a.at[vector_of(*step), pl.ds(0, wire)], recv_a.at[block, pl.ds(0, wire)],
-            a_s.at[i], a_r.at[i], task_peer(*step),
-        )
-        for i, step in enumerate(tasks)
-    ]
+
+    def arrive(p):
+        for d in range(1, N_Y):
+            their_rows = pl.ds(pl.multiple_of(lax.rem(y + N_Y - d, N_Y) * quarter, quarter), quarter)
+            pltpu.make_async_remote_copy(
+                src_ref=task_orb.at[their_rows, lane_pieces[p]], dst_ref=task_orb.at[their_rows, lane_pieces[p]],
+                send_sem=all_s.at[p, d - 1], recv_sem=all_r.at[p, d - 1], device_id={"slab": y_peer(d)},
+                device_id_type=MESH,
+            ).wait_recv()
+
+    copies = []
+    for p, (first, past, span) in enumerate(pieces):
+        arrive(p)
+        for i in span:
+            at = slice(i * 384, (i + 1) * 384)
+            orb = task_orb[:, at]
+            dense = dot(at_task, orb) * (1.0 / math.sqrt(occupied))
+            density[:, at] = dense
+            chosen = dot(pick, orb).astype(BF16)
+            pair = dense * (dot(target_points, chosen) * (1.0 / math.sqrt(targets_n)))
+            pair_1 = pair.astype(BF16)
+            rest = pair - pair_1.astype(F32)
+            pair_2 = rest.astype(BF16)
+            pair_3 = (rest - pair_2.astype(F32)).astype(BF16)
+            fitted = dot(fits, jnp.concatenate([pair_1, pair_2, pair_1, pair_3, pair_2, pair_1], axis=0))
+            for t in range(3):
+                flat[pl.ds(row_of(3 * i + t) - first, group, stride=PIECE), :] = fitted[:, t * LANES : (t + 1) * LANES]
+        send_a[:, first : first + PIECE, :] = flat[: N_GRID * PIECE, :].reshape(N_GRID, PIECE, LANES).astype(BF16)
+        copies.append(
+            [
+                push(
+                    send_a.at[vector_of(*step), pl.ds(first, past - first)],
+                    recv_a.at[block, pl.ds(first, past - first)],
+                    a_s.at[p, i], a_r.at[p, i], task_peer(*step),
+                )
+                for i, step in enumerate(tasks)
+            ]
+        )
     own = pltpu.make_async_copy(send_a.at[vector], recv_a.at[block], local)
     own.start()
     own.wait()
-    for copy in copies:
-        copy.wait()
+    for p, (first, past, span) in enumerate(pieces):
+        for copy in copies[p]:
+            copy.wait_recv()
+        flat[: N_GRID * PIECE, :] = recv_a[:, first : first + PIECE, :].astype(F32).reshape(N_GRID * PIECE, LANES)
+        for i in span:
+            for t in range(3):
+                packed[i * N_GRID : (i + 1) * N_GRID, t * LANES : (t + 1) * LANES] = flat[
+                    pl.ds(row_of(3 * i + t) - first, N_GRID, stride=PIECE), :
+                ].astype(BF16)
+    for copy in copies[0] + copies[1]:
+        copy.wait_send()
 
     @pl.when(away)
     def _():
-        fetch_orb.wait_send()
+        for copy in fetch_orb:
+            copy.wait_send()
 
     @pl.when(at_home)
     def _():
         for copy in hands:
             copy.wait_send()
 
-    flat[...] = recv_a[...].astype(F32).reshape(N_GRID * SLOT, LANES)
-
-    for i in range(rows):
-        for t in range(3):
-            packed[i * N_GRID : (i + 1) * N_GRID, t * LANES : (t + 1) * LANES] = flat[
-                pl.ds(row_of(3 * i + t), N_GRID, stride=SLOT), :
-            ].astype(BF16)
     for line in range(8):
         at = slice(line * LANES, (line + 1) * LANES)
         got = None
@@ -405,7 +439,7 @@
     own = pltpu.make_async_copy(send_b.at[block], recv_b.at[vector], local)
     own.start()
     own.wait()
-    sums = []
+    sums, over_y = [], []
     sender = hi * (N_LO // N_HI) + half
     for p, (first, past, span) in enumerate(pieces):
         for copy in spreads[p]:
@@ -416,15 +450,18 @@
             got = [flat[pl.ds(row_of(3 * i + t) - first, group, stride=PIECE), :] for t in range(3)]
             weighted = (jnp.concatenate(got, axis=1) * density[:, at]).astype(BF16)
             y_out[:, :, at] = dot(ordered, weighted).astype(BF16).reshape(N_Y, targets_n // N_Y, 384)
-        lanes = pl.ds(span[0] * 384, len(span) * 384)
-        copies = [
-            push(
-                y_out.at[lax.rem(y + d, N_Y), :, lanes], y_in.at[d - 1, :, lanes],
-                y_s.at[p, d - 1], y_r.at[p, d - 1], {"slab": y_peer(d)},
-            )
-            for d in range(1, N_Y)
-        ]
-        for copy in copies:
+        lanes = lane_pieces[p]
+        over_y.append(
+            [
+                push(
+                    y_out.at[lax.rem(y + d, N_Y), :, lanes], y_in.at[d - 1, :, lanes],
+                    y_s.at[p, d - 1], y_r.at[p, d - 1], {"slab": y_peer(d)},
+                )
+                for d in range(1, N_Y)
+            ]
+        )
+    for p, (first, past, span) in enumerate(pieces):
+        for copy in over_y[p]:
             copy.wait()
         for i in span:
             at = slice(i * 384, (i + 1) * 384)
@@ -517,8 +554,8 @@
             vmem((N_LO, each, SLOT, LANES), BF16),
             vmem((each * SLOT, LANES), F32),
             dma((near,)), dma((near,)), dma((far,)), dma((far,)),
-            dma, dma, dma((N_Y - 1,)), dma((N_Y - 1,)), dma((far,)), dma, dma((far,)), dma,
-            dma((peers,)), dma((peers,)), dma((2, peers)), dma((2, peers)),
+            dma((2,)), dma((2,)), dma((2, N_Y - 1)), dma((2, N_Y - 1)), dma((far,)), dma, dma((far,)), dma,
+            dma((2, peers)), dma((2, peers)), dma((2, peers)), dma((2, peers)),
             dma((2, N_Y - 1)), dma((2, N_Y - 1)), dma((2, N_LO)), dma((2, N_LO)), dma, dma((7,)),
         ],
         compiler_params=pltpu.CompilerParams(collective_id=0, has_side_effects=True, vmem_limit_bytes=60 * 1024 * 1024),

time: 111 us -> 108 us (0.973)
  Pallas kernels: 108 us -> 106 us
    pallas_call x1, Pallas kernels: 108 us -> 106 us  [body(): pl.pallas_call(functools.partial(kernel, occupied, targets_n, group, shar...]
where the time goes in v6:
time: 108 us; the launch traced here: 107 us
  Pallas kernels  106 us (98%)
  local copies, waits for them, and re-layouts  1.36 us (1%)
    pallas_call x1, Pallas kernels, body(): pl.pallas_call(functools.partial(kernel, occupied, targets_n, group, shar...  106 us

profile of v6, /device:TPU:6, one launch (start us, length us, event | category | flops | bytes accessed | tf_op | source)
XLA Modules:
  0.0 107.3 jit_solution(3192726349356149762)
XLA Ops:
  0.0 106.0 %exchange_operator.1 = f32[2,3456]{1,0:T(2,128)} custom-call(bf16[64,3456]{1,0:T(8,128)(2,1)} %orb_hbm.1, s32[1,64]{1,0:T(1,128)} %bitcast.2, s32[1,32]{1,0:T(1,128)} %bitcast.3, f32[32,32]{1,0:T(8,128)} %fit_hbm.1, bf16[2,48,144]{2,1,0:T(8,128)(2,1)} %constant.6.clone.left_hbm, bf16[96,128]{1,0:T(8,128)(2,1)} %constant.7.clone.lines_hbm, ...), custom_call_target="tpu_custom_call" | custom-call | tf_op jit(solution)/shard_map/exchange_operator/pallas_call | solution.py:518
  106.0 1.4 %copy.9 = f32[2,3456]{1,0:T(2,128)} copy(f32[2,3456]{1,0:T(2,128)} %exchange_operator.1) | data formatting | bytes 55296

commit v7 on v6

--- a/solution.py
+++ b/solution.py
@@ -234,6 +234,23 @@
     def _():
         for copy in keep_orb:
             copy.start()
+
+    def hand(source, target, send, recv):
+        return [
+            pltpu.make_async_remote_copy(
+                src_ref=source, dst_ref=target, send_sem=send.at[d - 1], recv_sem=recv,
+                device_id=task_peer(0, d, 0), device_id_type=MESH,
+            )
+            for d in range(1, N_HI)
+        ]
+
+    fit_hands = hand(fit_ref, task_fit, fit_s, fit_r)
+
+    @pl.when(at_home)
+    def _():
+        for copy in fit_hands:
+            copy.start()
+        task_fit[...] = fit_ref[...]
 
     near_steps = [(dx, 0, dc) for dx in range(N_X) for dc in range(N_CORE) if dx or dc]
     copies = [
@@ -257,23 +274,13 @@
     at_points = total.astype(BF16)
     home_at[...] = at_points
 
-    def hand(source, target, send, recv):
-        return [
-            pltpu.make_async_remote_copy(
-                src_ref=source, dst_ref=target, send_sem=send.at[d - 1], recv_sem=recv,
-                device_id=task_peer(0, d, 0), device_id_type=MESH,
-            )
-            for d in range(1, N_HI)
-        ]
-
-    hands = hand(home_at, task_at, at_s, at_r) + hand(fit_ref, task_fit, fit_s, fit_r)
+    hands = hand(home_at, task_at, at_s, at_r) + fit_hands
 
     @pl.when(at_home)
     def _():
-        for copy in hands:
+        for copy in hands[: N_HI - 1]:
             copy.start()
         task_at[...] = home_at[...]
-        task_fit[...] = fit_ref[...]
 
     copies = []
     for p, lanes in enumerate(lane_pieces):

time: 108 us -> 111 us (1.028)
  Pallas kernels: 106 us -> 108 us
    pallas_call x1, Pallas kernels: 106 us -> 108 us  [body(): pl.pallas_call(functools.partial(kernel, occupied, targets_n, group, shar...]
where the time goes in v7:
time: 111 us; the launch traced here: 110 us
  Pallas kernels  108 us (97%)
  local copies, waits for them, and re-layouts  1.36 us (1%)
    pallas_call x1, Pallas kernels, body(): pl.pallas_call(functools.partial(kernel, occupied, targets_n, group, shar...  108 us

profile of v7, /device:TPU:6, one launch (start us, length us, event | category | flops | bytes accessed | tf_op | source)
XLA Modules:
  0.0 109.6 jit_solution(12252298177714221662)
XLA Ops:
  0.0 108.2 %exchange_operator.1 = f32[2,3456]{1,0:T(2,128)} custom-call(bf16[64,3456]{1,0:T(8,128)(2,1)} %orb_hbm.1, s32[1,64]{1,0:T(1,128)} %bitcast.2, s32[1,32]{1,0:T(1,128)} %bitcast.3, f32[32,32]{1,0:T(8,128)} %fit_hbm.1, bf16[2,48,144]{2,1,0:T(8,128)(2,1)} %constant.6.clone.left_hbm, bf16[96,128]{1,0:T(8,128)(2,1)} %constant.7.clone.lines_hbm, ...), custom_call_target="tpu_custom_call" | custom-call | tf_op jit(solution)/shard_map/exchange_operator/pallas_call | solution.py:525
  108.2 1.4 %copy.9 = f32[2,3456]{1,0:T(2,128)} copy(f32[2,3456]{1,0:T(2,128)} %exchange_operator.1) | data formatting | bytes 55296
